TPU v7x, 32 devices: a whole 2x2x4 slice. The times are simulated.
32 devices in a mesh: seq: 16 (over z, x, core), head: 2 (over y).
Axes of the slice: x: 2, y: 2, z: 4, core: 2. Of those that a mesh axis runs over, the one named last changes fastest.
Arguments:
- features: bfloat16 [8, 32, 8, 512], P(None, 'seq', 'head'), may hold values from -540 to 540
- gn_gain: float32 [512], replicated, may hold values from 0.5 to 1.5
- gn_bias: float32 [512], replicated, may hold values from -3 to 3
- conv_weight: bfloat16 [3, 3, 3, 16, 512], replicated, may hold values from -0.0546875 to 0.0546875
- conv_bias: float32 [16], replicated, may hold values from -3 to 3
- patch_weight: bfloat16 [64, 3072], replicated, may hold values from -0.75 to 0.75
- patch_bias: float32 [3072], replicated, may hold values from -3 to 3
- image_mod: float32 [3, 3072], replicated, may hold values from -3 to 3
- w_qkv: bfloat16 [3072, 3, 2048], P('seq', None, 'head'), may hold values from -5 to 5
- text_ids: int32 [512], replicated, may hold values from 0 to 16383
- text_length: int32 [1], replicated, may hold values from 256 to 512
- text_table: bfloat16 [3072, 16384], P('seq'), may hold values from -60 to 60
- text_mod: float32 [2, 3072], P(None, 'seq'), may hold values from -3 to 3
- w_text: bfloat16 [3072, 2, 2048], P('seq', None, 'head'), may hold values from -2 to 2
- w_out: bfloat16 [2048, 3072], P('head'), may hold values from -0.625 to 0.625
- out_bias: float32 [3072], replicated, may hold values from -3 to 3
Outputs:
- block_out: bfloat16 [8, 16, 4, 3072], P(None, 'seq', 'head')
All inputs are finite; a program needn't handle non-finite values.
Results may differ from a plain program's by a relative error of at most 0.0089.
Values may be sent and summed in bfloat16 or wider, within the bound.
A program may use at most 128 MiB of HBM per device.

v0:
```python
import math

import jax
import jax.numpy as jnp
from jax import lax
from jax.sharding import PartitionSpec as P

HD = 128
GN_GROUPS = 32


eps_norm = 1e-06


def with_halo(cells, sides, width):
    for axis, dim in sides:
        count = lax.axis_size(axis)
        ends = count - 1
        head = lax.slice_in_dim(cells, 0, width, axis=dim)
        tail = lax.slice_in_dim(cells, cells.shape[dim] - width, cells.shape[dim], axis=dim)
        cells = jnp.concatenate(
            [
                lax.ppermute(tail, axis, [(i, (i + 1) % count) for i in range(ends)]),
                cells,
                lax.ppermute(head, axis, [((i + 1) % count, i) for i in range(ends)]),
            ],
            axis=dim,
        )
    return cells


def patchify(latent):
    frame_count, row_count, col_count, chan_count = latent.shape
    blocks = latent.reshape(frame_count, row_count // 2, 2, col_count // 2, 2, chan_count)
    blocks = blocks.transpose(0, 1, 3, 2, 4, 5)
    return blocks.reshape(frame_count * (row_count // 2) * (col_count // 2), 4 * chan_count)


def embed_tokens(patches, patch_weight, patch_bias, image_mod):
    hidden = jnp.dot(patches, patch_weight, preferred_element_type=jnp.float32) + patch_bias
    center = jnp.mean(hidden, axis=1, keepdims=True)
    offset = hidden - center
    spread = jnp.mean(offset * offset, axis=1, keepdims=True)
    normed = offset * lax.rsqrt(spread + eps_norm)
    modulated = (normed * (1.0 + image_mod[1]) + image_mod[0]).astype(jnp.bfloat16)
    return (hidden, modulated)


def text_start(query, text_keys, text_values, text_valid):
    scores = jnp.einsum("qhe,khe->qhk", query, text_keys, preferred_element_type=jnp.float32) / HD
    scores = jnp.where(text_valid[None, None, :], scores, -1e30)
    first_top = jnp.max(scores, axis=2)
    probs = jnp.exp(scores - first_top[..., None])
    first_total = jnp.sum(probs, axis=2)
    first_acc = jnp.einsum(
        "qhk,khe->qhe", probs.astype(jnp.bfloat16), text_values, preferred_element_type=jnp.float32
    )
    return (first_top, first_total, first_acc)


def attend_rows(query, state, piece):
    piece_rows = piece.shape[0]
    block_rows = math.gcd(piece_rows, 2048)
    heads_count = query.shape[1]
    blocks = piece.reshape(piece_rows // block_rows, block_rows, 2, heads_count, HD)

    def one_block(inner, block):
        run_top, run_total, run_acc = inner
        scores = (
            jnp.einsum("qhe,khe->qhk", query, block[:, 0], preferred_element_type=jnp.float32) / HD
        )
        new_top = jnp.maximum(run_top, jnp.max(scores, axis=2))
        factor = jnp.exp(run_top - new_top)
        probs = jnp.exp(scores - new_top[..., None])
        run_total = run_total * factor + jnp.sum(probs, axis=2)
        run_acc = run_acc * factor[..., None] + jnp.einsum(
            "qhk,khe->qhe",
            probs.astype(jnp.bfloat16),
            block[:, 1],
            preferred_element_type=jnp.float32,
        )
        return ((new_top, run_total, run_acc), None)

    return lax.scan(one_block, state, blocks)[0]


def body(
    features,
    gn_gain,
    gn_bias,
    conv_weight,
    conv_bias,
    patch_weight,
    patch_bias,
    image_mod,
    w_qkv,
    text_ids,
    text_length,
    text_table,
    text_mod,
    w_text,
    w_out,
    out_bias,
):
    frame_count, row_count, col_count, chan_count = features.shape
    width_full = patch_weight.shape[1]
    values = features.astype(jnp.float32)
    grouped = values.reshape(frame_count, row_count, col_count, GN_GROUPS, chan_count // GN_GROUPS)
    group_sums = jnp.sum(grouped, axis=(0, 1, 2, 4))
    group_squares = jnp.sum(grouped * grouped, axis=(0, 1, 2, 4))
    group_sums, group_squares = lax.psum((group_sums, group_squares), ("seq", "head"))
    cell_count = (
        frame_count
        * row_count
        * col_count
        * (chan_count // GN_GROUPS)
        * lax.axis_size("seq")
        * lax.axis_size("head")
    )
    group_mean = group_sums / cell_count
    group_scale = lax.rsqrt(group_squares / cell_count - group_mean * group_mean + eps_norm)
    normed = ((grouped - group_mean[:, None]) * group_scale[:, None]).reshape(
        frame_count, row_count, col_count, chan_count
    )
    activated = jax.nn.silu(normed * gn_gain + gn_bias).astype(jnp.bfloat16)
    rimmed = with_halo(activated, (("seq", 1), ("head", 2)), 1)
    padded = jnp.concatenate([rimmed[:1], rimmed[:1], rimmed], axis=0)
    windows = []
    for time_off in range(3):
        for row_off in range(3):
            for col_off in range(3):
                windows.append(
                    padded[
                        time_off : time_off + frame_count,
                        row_off : row_off + row_count,
                        col_off : col_off + col_count,
                    ]
                )
    stacked = jnp.stack(windows, axis=3)
    latent_chans = conv_weight.shape[3]
    kernels = conv_weight.reshape(27, latent_chans, chan_count)
    latent_sum = jnp.einsum("fyxkc,kzc->fyxz", stacked, kernels, preferred_element_type=jnp.float32)
    latent = (latent_sum + conv_bias).astype(jnp.bfloat16)
    patches = patchify(latent)
    hidden, own_modulated = embed_tokens(patches, patch_weight, patch_bias, image_mod)
    modulated = lax.all_gather(own_modulated, "head", axis=0, tiled=True)
    token_count = modulated.shape[0]
    head_width = w_qkv.shape[2]
    heads_here = head_width // HD
    qkv = jnp.einsum(
        "nd,dkj->nkj",
        modulated,
        lax.all_gather(w_qkv, "seq", axis=0, tiled=True),
        preferred_element_type=jnp.float32,
    ).astype(jnp.bfloat16)
    context = jnp.take(text_table, text_ids, axis=1).astype(jnp.float32)
    text_weight = w_text.astype(jnp.float32)
    text_gain = 1.0 + text_mod[1]
    text_shift = text_mod[0]
    text_sums, text_squares = lax.psum(
        (jnp.sum(context, axis=0), jnp.sum(context * context, axis=0)), "seq"
    )
    text_mean = text_sums / width_full
    text_scale = lax.rsqrt(text_squares / width_full - text_mean * text_mean + eps_norm)
    text_normed = (context - text_mean) * text_scale * text_gain[:, None] + text_shift[:, None]
    partial_kv = jnp.einsum(
        "dt,dkj->tkj", text_normed, text_weight, precision=lax.Precision.HIGHEST
    )
    text_kv = lax.psum(partial_kv, "seq")
    text_kv = text_kv.astype(jnp.bfloat16)
    text_count = text_kv.shape[0]
    text_valid = jnp.arange(text_count, dtype=jnp.int32) < text_length[0]
    query = qkv[:, 0].reshape(token_count, heads_here, HD)
    text_keys = text_kv[:, 0].reshape(text_count, heads_here, HD)
    text_values = text_kv[:, 1].reshape(text_count, heads_here, HD)
    first_state = text_start(query, text_keys, text_values, text_valid)
    image_kv = qkv[:, 1:3]
    run_top, run_total, run_acc = attend_rows(
        query, first_state, lax.all_gather(image_kv, "seq", axis=0, tiled=True)
    )
    attended = (
        (run_acc / run_total[..., None]).astype(jnp.bfloat16).reshape(token_count, head_width)
    )
    projected = (
        lax.psum_scatter(
            jnp.dot(attended, w_out, preferred_element_type=jnp.float32),
            "head",
            scatter_dimension=0,
            tiled=True,
        )
        + out_bias
    )
    block_out = (hidden + image_mod[2] * projected).astype(jnp.bfloat16)
    return block_out.reshape(frame_count, row_count // 2, col_count // 2, width_full)


def solution(mesh):
    return jax.shard_map(
        body,
        mesh=mesh,
        in_specs=(
            P(None, "seq", "head", None),
            P(),
            P(),
            P(),
            P(),
            P(),
            P(),
            P(),
            P("seq", None, "head"),
            P(),
            P(),
            P("seq", None),
            P(None, "seq"),
            P("seq", None, "head"),
            P("head", None),
            P(),
        ),
        out_specs=P(None, "seq", "head", None),
        check_vma=False,
    )
```

profile of v0, /device:TPU:0, one launch (start us, length us, event | category | flops | bytes accessed | tf_op | source)
XLA Modules:
  0.0 285.2 jit_solution(11076966553390359524)
XLA Ops:
  6.5 0.7 all-gather.3.cloned.1.call-update
  7.3 0.9 convert_reduce_fusion.1
  8.6 43.1 %all-reduce = (f32[32]{0:T(128)S(1)}, f32[32]{0:T(128)S(1)}) all-reduce(f32[32]{0:T(128)S(1)} %reduce_sum.92, f32[32]{0:T(128)S(1)} %reduce_sum.89), channel_id=1, replica_groups=mesh['seq'=16,'head'=2] {'seq','head'}, use_global_device_ids=true, to_apply=%region_5.6 | all-reduce | flops 64 | bytes 512 | tf_op jit(solution)/shard_map/psum | solution.py:111
  52.0 1.0 fusion.41
  52.9 1.8 collective-permute-start
  54.7 1.3 collective-permute-start.1
  56.0 0.7 compare_select_fusion
  56.7 1.0 fusion.78
  57.7 0.7 compare_and_fusion
  58.4 1.5 collective-permute-done.1
  59.9 2.5 collective-permute-start.2
  62.4 1.3 collective-permute-start.3
  63.7 10.1 %copy.82 = bf16[192,16384]{0,1:T(8,128)(2,1)} copy(bf16[192,16384]{1,0:T(8,128)(2,1)} %param.27) | data formatting | bytes 12582912 | tf_op args[11]
  73.8 6.2 %gather_fusion = bf16[512,192]{1,0:T(8,128)(2,1)S(1)} fusion(bf16[192,16384]{0,1:T(8,128)(2,1)} %copy.82, s32[1024]{0:T(1024)S(1)} %pad_clamp_fusion), kind=kCustom, calls=%fused_computation | custom fusion | bytes 395264 | tf_op jit(solution)/shard_map/jit(_take)/gather | solution.py:156
  81.6 0.6 fusion.9
  82.9 5.9 %all_gather.9 = bf16[32,3072]{1,0:T(8,128)(2,1)S(1)} all-gather(bf16[16,3072]{1,0:T(8,128)(2,1)S(1)} %add_convert_fusion.1), channel_id=1, replica_groups=mesh['seq'=16,'head'=2] {'head'}, dimensions={0}, use_global_device_ids=true | all-gather | bytes 294912 | tf_op jit(solution)/shard_map/all_gather | solution.py:146
  88.8 23.2 %all-gather.3.cloned.1.call-done = bf16[3072,3,1024]{2,0,1:T(8,128)(2,1)} async-done(((bf16[192,3,1024]{2,0,1:T(8,128)(2,1)}), bf16[3072,3,1024]{2,0,1:T(8,128)(2,1)}) %all-gather.3.cloned.1.call-update) | async-done | bytes 18874384 | tf_op jit(solution)/shard_map/all_gather | solution.py:153
  112.0 9.7 %convolution_convert_fusion = bf16[32,3,1024]{2,0,1:T(8,128)(2,1)S(1)} fusion(bf16[3072,3,1024]{2,0,1:T(8,128)(2,1)} %all-gather.3.cloned.1.call-done, bf16[32,3072]{1,0:T(8,128)(2,1)S(1)} %all_gather.9), kind=kOutput, calls=%fused_computation.7 | convolution fusion | flops 604078080 | bytes 19267584 | tf_op jit(solution)/shard_map/nd,dkj->nkj/dot_general | solution.py:150
  121.7 0.7 slice.219
  122.8 33.0 %all-reduce.1 = (f32[512]{0:T(512)S(1)}, f32[512]{0:T(512)S(1)}) all-reduce(f32[512]{0:T(512)S(1)} %get-tuple-element.16, f32[512]{0:T(512)S(1)} %get-tuple-element.15), channel_id=1, replica_groups=mesh['seq'=16,'head'=2] {'seq'}, use_global_device_ids=true, to_apply=%region_9.10 | all-reduce | flops 1024 | bytes 8192 | tf_op jit(solution)/shard_map/psum | solution.py:160
  155.8 3.9 %fusion.12 = f32[512,2,1024]{2,0,1:T(8,128)} fusion(bf16[192,2,1024]{2,1,0:T(2,128)(2,1)S(1)} %copy-done, f32[192]{0:T(256)S(1)} %bitcast.263, f32[192]{0:T(256)S(1)} %bitcast.262, f32[512]{0:T(512)S(1)} %get-tuple-element.47, f32[512]{0:T(512)S(1)} %get-tuple-element.46, bf16[512,192]{1,0:T(8,128)(2,1)S(1)} %gather_fusion, ...), kind=kOutput, calls=%fused_computation.24 | convolution fusion | flops 2416508928 | bytes 5183488 | tf_op jit(solution)/shard_map/dt,dkj->tkj/dot_general | solution.py:166
  159.7 94.6 %all-reduce.3 = bf16[512,2,1024]{2,0,1:T(8,128)(2,1)S(1)} all-reduce(f32[512,2,1024]{2,0,1:T(8,128)} %fusion.12), channel_id=1, replica_groups=mesh['seq'=16,'head'=2] {'seq'}, use_global_device_ids=true, to_apply=%region_10.11 | all-reduce | flops 1048576 | bytes 6291456 | tf_op jit(solution)/shard_map/psum | solution.py:169
  255.8 1.3 fusion.80
  257.0 2.4 copy.103
  259.6 0.6 fusion.81
  260.1 0.6 copy-done.2
  261.1 0.4 convolution_bitcast_fusion
  261.5 0.4 fusion.7
  261.9 1.9 fusion.43
  263.9 13.2 %reduce-scatter.2.cloned.1.call-done = f32[16,3072]{1,0:T(8,128)} async-done(((f32[32,3072]{1,0:T(8,128)}), f32[16,3072]{1,0:T(8,128)}) %reduce-scatter.2.cloned.1.call-update) | async-done | bytes 196624 | tf_op jit(solution)/shard_map/reduce_scatter | solution.py:185
  277.1 1.0 add_convert_fusion
  278.0 0.7 reshape.87
  (98 shorter events, 4.4 us)
Async XLA Ops:
  6.5 149.3 %copy-start = (bf16[192,2,1024]{2,1,0:T(2,128)(2,1)S(1)}, bf16[192,2,1024]{2,1,0:T(2,128)(2,1)}, u32[]{:S(2)}) copy-start(bf16[192,2,1024]{2,1,0:T(2,128)(2,1)} %param.29) | copy-start | bytes 2359300
  6.5 105.4 %all-gather.3.cloned.1.call-start = ((), (), s32[]{:S(2)}) async-start(), calls=%async_computation.1 | async-start | bytes 20054016 | tf_op jit(solution)/shard_map/all_gather | solution.py:153
  7.3 249.8 %all-gather.5.cloned.1.call-start = ((), (), s32[]{:S(2)}) async-start(), calls=%async_computation.2 | async-start | bytes 2228224 | tf_op jit(solution)/shard_map/all_gather | solution.py:179
  52.9 5.4 %collective-permute-start = (bf16[8,1,4,512]{3,0,2,1:T(8,128)(2,1)S(1)}, bf16[8,1,4,512]{3,0,2,1:T(8,128)(2,1)S(1)}, u32[]{:S(2)}, u32[]{:S(2)}) collective-permute-start(bf16[8,1,4,512]{3,0,2,1:T(8,128)(2,1)S(1)} %get-tuple-element.41), channel_id=1, source_target_pairs={{0,2},{2,4},{4,6},{6,8},{8,10},{10,12},{12,14},{14,16},{16,18},{18... | collective-permute-start | bytes 98312 | tf_op jit(solution)/shard_map/ppermute | solution.py:23
  54.7 5.2 %collective-permute-start.1 = (bf16[8,1,4,512]{3,0,2,1:T(8,128)(2,1)S(1)}, bf16[8,1,4,512]{3,0,2,1:T(8,128)(2,1)S(1)}, u32[]{:S(2)}, u32[]{:S(2)}) collective-permute-start(bf16[8,1,4,512]{3,0,2,1:T(8,128)(2,1)S(1)} %get-tuple-element.42), channel_id=1, source_target_pairs={{2,0},{4,2},{6,4},{8,6},{10,8},{12,10},{14,12},{16,14},{18,16},{20... | collective-permute-start | bytes 98312 | tf_op jit(solution)/shard_map/ppermute | solution.py:25
  59.9 20.1 %collective-permute-start.2 = (bf16[8,4,1,512]{3,0,2,1:T(8,128)(2,1)S(1)}, bf16[8,4,1,512]{3,0,2,1:T(8,128)(2,1)S(1)}, u32[]{:S(2)}, u32[]{:S(2)}) collective-permute-start(bf16[8,4,1,512]{3,0,2,1:T(8,128)(2,1)S(1)} %get-tuple-element.39), channel_id=1, source_target_pairs={{0,1},{2,3},{4,5},{6,7},{8,9},{10,11},{12,13},{14,15},{16,17},{18,... | collective-permute-start | bytes 98312 | tf_op jit(solution)/shard_map/ppermute | solution.py:23
  62.4 17.6 %collective-permute-start.3 = (bf16[8,4,1,512]{3,0,2,1:T(8,128)(2,1)S(1)}, bf16[8,4,1,512]{3,0,2,1:T(8,128)(2,1)S(1)}, u32[]{:S(2)}, u32[]{:S(2)}) collective-permute-start(bf16[8,4,1,512]{3,0,2,1:T(8,128)(2,1)S(1)} %get-tuple-element.40), channel_id=1, source_target_pairs={{1,0},{3,2},{5,4},{7,6},{9,8},{11,10},{13,12},{15,14},{17,16},{19,... | collective-permute-start | bytes 98312 | tf_op jit(solution)/shard_map/ppermute | solution.py:25
  80.3 0.8 copy-start.1
  80.4 0.8 copy-start.7
  80.4 0.8 copy-start.8
  80.5 1.0 copy-start.3
  80.5 1.0 copy-start.9
  80.8 1.5 copy-start.4
  80.8 1.5 copy-start.5
  88.8 67.0 %copy-start.10 = (f32[2,192]{1,0:T(2,128)S(1)}, f32[2,192]{1,0:T(2,128)}, u32[]{:S(2)}) copy-start(f32[2,192]{1,0:T(2,128)} %param.28) | copy-start | bytes 4612
  122.4 154.7 %reduce-scatter.2.cloned.1.call-start = ((), (), s32[]{:S(2)}) async-start(), calls=%async_computation.3 | async-start | bytes 589824 | tf_op jit(solution)/shard_map/reduce_scatter | solution.py:185
  257.0 4.9 %slice-start = ((s8[6291456]{0:T(1024)(128)(4,1)}), s8[4194304]{0:T(1024)(128)(4,1)S(1)}, s32[]{:S(2)}) async-start(s8[6291456]{0:T(1024)(128)(4,1)} %bitcast.249), calls=%async_computation.4 | async-start | bytes 8388608
  259.4 2.5 slice-start.1
  259.6 1.2 copy-start.2
  261.9 15.2 %copy-start.6 = (f32[3072]{0:T(1024)S(1)}, f32[3072]{0:T(1024)}, u32[]{:S(2)}) copy-start(f32[3072]{0:T(1024)} %param.31) | copy-start | bytes 36868
Sparse Core Ops, SparseCore 0:
  8.9 103.0 all-gather.2
  122.5 42.3 all-gather.4
  264.0 12.9 reduce-scatter.1
where the time goes:
time: 286 us; the launch traced here: 285 us
  blocking collectives  177 us (62%)
  waiting for transfers between devices  38.6 us (13%)
  local copies, waits for them, and re-layouts  22.7 us (8%)
  matrix products  19.1 us (7%)
  between operations  14.3 us (5%)
  starting transfers between devices  6.94 us (2%)
  other arithmetic  6.94 us (2%)
    psum x1, blocking collectives, body(): text_kv = lax.psum(partial_kv, 'seq')  94.6 us
    psum x1, blocking collectives, body(): lax.psum((group_sums, group_squares), ('seq', 'head'))  43.1 us
    psum x1, blocking collectives, body(): lax.psum((jnp.sum(context, axis=0), jnp.sum(context * context, axis=0)),...  33 us
    all_gather x1, waiting for transfers between devices, body(): lax.all_gather(w_qkv, 'seq', axis=0, tiled=True)  23.2 us
    unnamed x56, local copies, waits for them, and re-layouts  14.5 us
    reduce_scatter x1, waiting for transfers between devices, body(): lax.psum_scatter(jnp.dot(attended, w_out, preferred_element_type=jnp.floa...  13.2 us
    dot_general x1, matrix products, body(): jnp.einsum('nd,dkj->nkj', modulated, lax.all_gather(w_qkv, 'seq', axis=0,...  9.7 us
    gather x1, local copies, waits for them, and re-layouts, body(): context = jnp.take(text_table, text_ids, axis=1).astype(jnp.float32)  6.18 us
  transfers between devices with their start and end apart: 7, of which 3 were waited for; matrix products, arithmetic and copies ran while one was open for 10% of the time, Pallas kernels for 0%

commit v1 on v0

v1 whole, which is shorter than its diff:
```python
import jax
import jax.numpy as jnp
from jax import lax
from jax.sharding import PartitionSpec as P

HD = 128
GN_GROUPS = 32
CHUNK = 512

eps_norm = 1e-06


def group_gather(piece, group, dim):
    if group == 1:
        return piece
    count = lax.axis_size("seq")
    if group == 2:
        other = lax.ppermute(piece, "seq", [(i, i ^ 1) for i in range(count)])
        first = lax.axis_index("seq") % 2 == 0
        return jnp.concatenate(
            [jnp.where(first, piece, other), jnp.where(first, other, piece)], axis=dim
        )
    members = [list(range(i, i + group)) for i in range(0, count, group)]
    return lax.all_gather(piece, "seq", axis=dim, tiled=True, axis_index_groups=members)


def group_norm(features, gn_gain, gn_bias):
    frame_count, row_count, col_count, chan_count = features.shape
    per_group = chan_count // GN_GROUPS
    values = features.astype(jnp.float32)
    chan_sums = jnp.stack(
        [jnp.sum(values, axis=(0, 1, 2)), jnp.sum(values * values, axis=(0, 1, 2))]
    )
    sums = jnp.sum(chan_sums.reshape(2, GN_GROUPS, per_group), axis=2)
    sums = lax.psum(sums, ("seq", "head"))
    cell_count = (
        frame_count * row_count * col_count * per_group * lax.axis_size("seq") * lax.axis_size("head")
    )
    mean = sums[0] / cell_count
    scale = lax.rsqrt(sums[1] / cell_count - mean * mean + eps_norm)
    mean = jnp.repeat(mean, per_group)
    scale = jnp.repeat(scale, per_group)
    normed = (values - mean) * scale
    return jax.nn.silu(normed * gn_gain + gn_bias).astype(jnp.bfloat16)


def join_rims(parts, block_dim, dim, unit):
    size = parts.shape[dim]
    blocks = parts.shape[block_dim]
    core = lax.slice_in_dim(parts, unit, size - unit, axis=dim)
    low = lax.slice_in_dim(parts, 0, unit, axis=dim)
    high = lax.slice_in_dim(parts, size - unit, size, axis=dim)
    low = lax.slice_in_dim(low, 1, blocks, axis=block_dim)
    high = lax.slice_in_dim(high, 0, blocks - 1, axis=block_dim)
    pad_low = [(0, 0)] * parts.ndim
    pad_low[block_dim] = (0, 1)
    pad_low[dim] = (size - 3 * unit, 0)
    pad_high = [(0, 0)] * parts.ndim
    pad_high[block_dim] = (1, 0)
    pad_high[dim] = (0, size - 3 * unit)
    return core + jnp.pad(low, pad_low) + jnp.pad(high, pad_high)


def all_patches(activated, conv_weight, conv_bias):
    seq_n, head_n = lax.axis_size("seq"), lax.axis_size("head")
    frame_count, row_count, col_count, _ = activated.shape
    chans = conv_weight.shape[3]
    padded = jnp.concatenate([activated[:1], activated[:1], activated], axis=0)
    shares = lax.conv_general_dilated(
        padded[None],
        conv_weight,
        (1, 1, 1),
        ((0, 0), (2, 2), (2, 2)),
        dimension_numbers=("NDHWC", "DHWOI", "NDHWC"),
        preferred_element_type=jnp.float32,
    )[0]
    flat = shares.reshape(-1, 128)
    parts = lax.all_gather(flat, ("seq", "head"), axis=0, tiled=False)
    parts = parts.reshape(
        seq_n, head_n, frame_count, row_count + 2, (col_count + 2) * chans
    )
    parts = join_rims(join_rims(parts, 0, 3, 1), 1, 4, chans)
    latent = (parts + jnp.tile(conv_bias, col_count)).astype(jnp.bfloat16)
    blocks = latent.reshape(
        seq_n, head_n, frame_count, row_count // 2, 2, col_count // 2, 2 * chans
    )
    blocks = blocks.transpose(0, 1, 2, 3, 5, 4, 6)
    own = frame_count * (row_count // 2) * (col_count // 2)
    return blocks.reshape(seq_n * head_n * own, 4 * chans)


def modulate(patches, patch_weight, patch_bias, image_mod):
    hidden = jnp.dot(patches, patch_weight, preferred_element_type=jnp.float32) + patch_bias
    center = jnp.mean(hidden, axis=1, keepdims=True)
    offset = hidden - center
    spread = jnp.mean(offset * offset, axis=1, keepdims=True)
    normed = offset * lax.rsqrt(spread + eps_norm)
    return (normed * (1.0 + image_mod[1]) + image_mod[0]).astype(jnp.bfloat16)


def body(
    features,
    gn_gain,
    gn_bias,
    conv_weight,
    conv_bias,
    patch_weight,
    patch_bias,
    image_mod,
    w_qkv,
    text_ids,
    text_length,
    text_table,
    text_mod,
    w_text,
    w_out,
    out_bias,
):
    frame_count, row_count, col_count, _ = features.shape
    width_full = patch_weight.shape[1]
    seq_n, head_n = lax.axis_size("seq"), lax.axis_size("head")
    seq_i, head_i = lax.axis_index("seq"), lax.axis_index("head")
    depth, _, head_width = w_qkv.shape
    heads_here = head_width // HD
    group = seq_n // heads_here
    cols = head_width // seq_n
    text_count = text_ids.shape[0]

    both = jnp.concatenate([w_qkv, w_text], axis=1).reshape(depth, 5, seq_n, cols)
    both = both.transpose(2, 0, 1, 3).reshape(seq_n, depth, 5 * cols)
    both = lax.all_to_all(both, "seq", split_axis=0, concat_axis=0, tiled=True)
    both = both.reshape(seq_n * depth, 5, cols)
    both = group_gather(both, group, 2)
    w_query, w_image, w_text_full = both[:, 0], both[:, 1:3], both[:, 3:5]

    chosen = (
        lax.broadcasted_iota(jnp.int32, (text_table.shape[1], text_count), 0) == text_ids[None, :]
    ).astype(jnp.bfloat16)
    own_context = jnp.dot(text_table, chosen, preferred_element_type=jnp.float32).astype(
        jnp.bfloat16
    )
    context = lax.all_gather(own_context, "seq", axis=0, tiled=True).astype(jnp.float32)
    mod = lax.all_gather(text_mod, "seq", axis=1, tiled=True)
    text_mean = jnp.sum(context, axis=0) / width_full
    text_square = jnp.sum(context * context, axis=0) / width_full
    text_scale = lax.rsqrt(text_square - text_mean * text_mean + eps_norm)
    text_normed = (context - text_mean) * text_scale * (1.0 + mod[1][:, None]) + mod[0][:, None]
    text_high = text_normed.astype(jnp.bfloat16)
    text_low = (text_normed - text_high.astype(jnp.float32)).astype(jnp.bfloat16)
    w_text_flat = w_text_full.reshape(width_full, 2 * HD)
    text_kv = sum(
        lax.dot_general(
            part, w_text_flat, (((0,), (0,)), ((), ())), preferred_element_type=jnp.float32
        )
        for part in (text_high, text_low)
    ).astype(jnp.bfloat16)

    activated = group_norm(features, gn_gain, gn_bias)
    patches = all_patches(activated, conv_weight, conv_bias)
    own = patches.shape[0] // (seq_n * head_n)
    part_rows = head_n * own // group
    my_part = seq_i % group
    chunk = min(CHUNK, patches.shape[0])

    def project(rows):
        modulated = modulate(rows, patch_weight, patch_bias, image_mod)
        kv = jnp.dot(
            modulated, w_image.reshape(width_full, 2 * HD), preferred_element_type=jnp.float32
        )
        query = jnp.dot(modulated, w_query, preferred_element_type=jnp.float32)
        query = lax.dynamic_index_in_dim(
            query.reshape(-1, group, part_rows, HD), my_part, axis=1, keepdims=False
        )
        return kv.astype(jnp.bfloat16), query.reshape(-1, HD).astype(jnp.bfloat16)

    if chunk == patches.shape[0]:
        image_kv, query = project(patches)
    else:
        image_kv, query = lax.map(project, patches.reshape(-1, chunk, patches.shape[1]))
        image_kv = image_kv.reshape(-1, 2 * HD)
        query = query.reshape(-1, HD)

    keys = jnp.concatenate([image_kv[:, :HD], text_kv[:, :HD]], axis=0)
    vals = jnp.concatenate([image_kv[:, HD:], text_kv[:, HD:]], axis=0)
    key_valid = (
        jnp.arange(keys.shape[0], dtype=jnp.int32) < image_kv.shape[0] + text_length[0]
    )
    scores = (
        lax.dot_general(query, keys, (((1,), (1,)), ((), ())), preferred_element_type=jnp.float32)
        / HD
    )
    scores = jnp.where(key_valid[None, :], scores, -1e30)
    probs = jnp.exp(scores - jnp.max(scores, axis=1, keepdims=True))
    totals = jnp.sum(probs, axis=1, keepdims=True)
    attended = (
        jnp.dot(probs.astype(jnp.bfloat16), vals, preferred_element_type=jnp.float32) / totals
    ).astype(jnp.bfloat16)

    attended = attended.reshape(seq_n, part_rows, HD)
    attended = lax.all_to_all(attended, "seq", split_axis=0, concat_axis=0, tiled=True)
    attended = attended.reshape(heads_here, group, part_rows, HD).transpose(1, 2, 0, 3)
    attended = attended.reshape(head_n * own, head_width)
    if head_n == 2:
        halves = attended.reshape(2, own, head_width)
        away = jnp.dot(
            lax.dynamic_index_in_dim(halves, 1 - head_i, 0, keepdims=False),
            w_out,
            preferred_element_type=jnp.float32,
        )
        here = jnp.dot(
            lax.dynamic_index_in_dim(halves, head_i, 0, keepdims=False),
            w_out,
            preferred_element_type=jnp.float32,
        )
        projected = here + lax.ppermute(away, "head", [(0, 1), (1, 0)]) + out_bias
    else:
        projected = (
            lax.psum_scatter(
                jnp.dot(attended, w_out, preferred_element_type=jnp.float32),
                "head",
                scatter_dimension=0,
                tiled=True,
            )
            + out_bias
        )
    own_patches = lax.dynamic_slice_in_dim(patches, (seq_i * head_n + head_i) * own, own, axis=0)
    hidden = jnp.dot(own_patches, patch_weight, preferred_element_type=jnp.float32) + patch_bias
    block_out = (hidden + image_mod[2] * projected).astype(jnp.bfloat16)
    return block_out.reshape(frame_count, row_count // 2, col_count // 2, width_full)


def solution(mesh):
    return jax.shard_map(
        body,
        mesh=mesh,
        in_specs=(
            P(None, "seq", "head", None),
            P(),
            P(),
            P(),
            P(),
            P(),
            P(),
            P(),
            P("seq", None, "head"),
            P(),
            P(),
            P("seq", None),
            P(None, "seq"),
            P("seq", None, "head"),
            P("head", None),
            P(),
        ),
        out_specs=P(None, "seq", "head", None),
        check_vma=False,
    )
```

time: 286 us -> 297 us (1.038)
  waiting for transfers between devices: 38.6 us -> 12.4 us
  matrix products: 19.1 us -> 37.4 us
  other arithmetic: 6.94 us -> 21.1 us
  blocking collectives: 177 us -> 169 us
  local copies, waits for them, and re-layouts: 22.7 us -> 29.8 us
  starting transfers between devices: 6.94 us -> 11.4 us
    psum x3 -> x1, blocking collectives: 171 us -> 83.9 us  [group_norm(): sums = lax.psum(sums, ('seq', 'head'))]
    all_gather x1 -> x2, blocking collectives: 5.88 us -> 85.6 us  [the longest x1 68.1 us: all_patches(): parts = lax.all_gather(flat, ('seq', 'head'), axis=0, tiled=False)]
    all_gather x2 -> x1, waiting for transfers between devices: 23.2 us -> 0.02 us  [body(): lax.all_gather(own_context, 'seq', axis=0, tiled=True).astype(jnp.float32)]
    dot_general x9 -> x11, matrix products: 19.1 us -> 33.1 us  [the longest x1 9.15 us: body(): jnp.dot(text_table, chosen, preferred_element_type=jnp.float32)]
    reduce_scatter x1 -> x0, waiting for transfers between devices: 13.2 us -> none  [body(): lax.psum_scatter(jnp.dot(attended, w_out, preferred_element_type=jnp.floa...]
    all_to_all x0 -> x2, starting transfers between devices: none -> 11 us  [the longest x1 7.4 us: body(): both = lax.all_to_all(both, 'seq', split_axis=0, concat_axis=0, tiled=True)]
    reshape x2 -> x6, local copies, waits for them, and re-layouts: 0.1 us -> 10.1 us  [the longest x2 6.84 us: body(): both = both.reshape(seq_n * depth, 5, cols)]
    unnamed x56 -> x43, local copies, waits for them, and re-layouts: 14.5 us -> 4.71 us
  transfers between devices with their start and end apart: 7 -> 5, of which waited for: 3 -> 2; matrix products, arithmetic and copies ran while one was open for 10% -> 21% of each run, Pallas kernels for 0% -> 0%
where the time goes in v1:
time: 297 us; the launch traced here: 296 us
  blocking collectives  169 us (57%)
  matrix products  37.4 us (13%)
  local copies, waits for them, and re-layouts  29.8 us (10%)
  other arithmetic  21.1 us (7%)
  between operations  14.6 us (5%)
  waiting for transfers between devices  12.4 us (4%)
  starting transfers between devices  11.4 us (4%)
    psum x1, blocking collectives, group_norm(): sums = lax.psum(sums, ('seq', 'head'))  83.9 us
    all_gather x1, blocking collectives, all_patches(): parts = lax.all_gather(flat, ('seq', 'head'), axis=0, tiled=False)  68.1 us
    all_gather x1, blocking collectives, body(): mod = lax.all_gather(text_mod, 'seq', axis=1, tiled=True)  17.4 us
    dot_general x1, matrix products, body(): jnp.dot(text_table, chosen, preferred_element_type=jnp.float32)  9.15 us
    all_to_all x1, starting transfers between devices, body(): both = lax.all_to_all(both, 'seq', split_axis=0, concat_axis=0, tiled=True)  7.4 us
    all_to_all x1, waiting for transfers between devices, body(): lax.all_to_all(attended, 'seq', split_axis=0, concat_axis=0, tiled=True)  6.85 us
    reshape x2, local copies, waits for them, and re-layouts, body(): both = both.reshape(seq_n * depth, 5, cols)  6.84 us
    convert_element_type x1, other arithmetic, modulate(): return (normed * (1.0 + image_mod[1]) + image_mod[0]).astype(jnp.bfloat16)  6.3 us
  transfers between devices with their start and end apart: 5, of which 2 were waited for; matrix products, arithmetic and copies ran while one was open for 21% of the time, Pallas kernels for 0%

profile of v1, /device:TPU:0, one launch (start us, length us, event | category | flops | bytes accessed | tf_op | source)
XLA Modules:
  0.0 296.0 jit_solution(9451545067675089896)
XLA Ops:
  6.5 2.5 copy.83
  9.0 1.6 copy.82
  11.3 2.6 copy.85
  13.9 7.4 %all-to-all-start = ((bf16[16,192,320]{2,1,0:T(8,128)(2,1)}), bf16[16,192,320]{2,1,0:T(8,128)(2,1)}, u32[]{:S(2)}, u32[]{:S(2)}) async-start(bf16[16,192,320]{2,1,0:T(8,128)(2,1)} %copy.85), calls=%async_computation | async-start | bytes 4718592 | tf_op jit(solution)/shard_map/all_to_all | solution.py:131
  21.5 9.1 %fusion.23 = bf16[192,512]{1,0:T(8,128)(2,1)} fusion(bf16[192,16384]{1,0:T(8,128)(2,1)} %param.27, s32[512]{0:T(512)S(1)} %copy-done.19), kind=kOutput, calls=%fused_computation.34 | convolution fusion | flops 3229712384 | bytes 6490112 | tf_op jit(solution)/shard_map/dot_general | solution.py:139
  31.0 83.9 %psum.7 = f32[2,32]{1,0:T(2,128)S(1)} all-reduce(f32[2,32]{1,0:T(2,128)S(1)} %maximum_reduce_fusion), channel_id=1, replica_groups=mesh['seq'=16,'head'=2] {'seq','head'}, use_global_device_ids=true, to_apply=%region_3.4 | all-reduce | flops 64 | bytes 512 | tf_op jit(solution)/shard_map/psum | solution.py:35
  115.4 4.2 %convolution_reduce_fusion = f32[8,4,6,16]{3,2,1,0:T(8,128)S(1)} fusion(bf16[3,3,3,16,512]{4,3,2,1,0:T(8,128)(2,1)S(1)} %copy-done, bf16[1,10,2,4,512]{4,3,2,1,0:T(4,128)(2,1)S(1)} %maximum_bitcast_fusion.2), kind=kOutput, calls=%fused_computation.36 | convolution fusion | flops 28311552 | bytes 536576 | tf_op jit(solution)/shard_map/conv_general_dilated | solution.py:69
  119.7 68.1 %all_gather.9 = f32[32,24,128]{2,1,0:T(8,128)S(1)} all-gather(f32[1,24,128]{2,1,0:T(8,128)S(1)} %all_gather_reshape_squeeze.3), channel_id=1, replica_groups=mesh['seq'=16,'head'=2] {'seq','head'}, dimensions={0}, use_global_device_ids=true | all-gather | bytes 405504 | tf_op jit(solution)/shard_map/all_gather | solution.py:78
  189.6 3.6 %add_reduce_fusion = (f32[512]{0:T(512)S(1)}, f32[512,3072]{1,0:T(8,128)}) fusion(f32[3072]{0:T(1024)S(1)} %copy-done.11, bf16[512,64]{1,0:T(8,128)(2,1)S(1)} %reshape.100, bf16[64,3072]{1,0:T(8,128)(2,1)S(1)} %copy-done.7), kind=kOutput, calls=%fused_computation.15 | convolution fusion | flops 204471808 | bytes 6764544 | tf_op jit(solution)/shard_map/dot_general | solution.py:93
  193.2 17.4 %all-gather = f32[16,192,2]{1,2,0:T(2,128)S(1)} all-gather(f32[1,192,2]{1,2,0:T(2,128)S(1)} %bitcast.101), channel_id=1, replica_groups=mesh['seq'=16,'head'=2] {'seq'}, dimensions={0}, use_global_device_ids=true | all-gather | bytes 26112 | tf_op jit(solution)/shard_map/all_gather | solution.py:143
  210.8 3.9 %copy.86 = bf16[16,192,320]{1,0,2:T(8,128)(2,1)S(1)} copy(bf16[16,192,320]{2,1,0:T(8,128)(2,1)} %all-to-all-done) | data formatting | bytes 3932160 | tf_op jit(solution)/shard_map/all_to_all | solution.py:131
  214.7 3.7 %reshape.103 = bf16[3072,5,64]{0,2,1:T(8,128)(2,1)} reshape(bf16[16,192,320]{1,0,2:T(8,128)(2,1)S(1)} %copy.86) | data formatting | bytes 3932160 | tf_op jit(solution)/shard_map/reshape | solution.py:132
  218.7 3.7 %multiply_reduce_fusion = f32[512]{0:T(512)S(1)} fusion(f32[512,3072]{1,0:T(8,128)} %get-tuple-element.29, f32[512]{0:T(512)S(1)} %broadcast_multiply_fusion.1, f32[3072]{0:T(1024)S(1)} %copy-done.11), kind=kLoop, calls=%fused_computation.14 | loop fusion | flops 6290944 | bytes 6307840 | tf_op jit(solution)/shard_map/reduce_sum | solution.py:96
  223.2 6.3 %add_convert_fusion = bf16[512,3072]{1,0:T(8,128)(2,1)} fusion(f32[512,3072]{1,0:T(8,128)} %get-tuple-element.29, f32[3072]{0:T(1024)S(1)} %bitcast.95, f32[3072]{0:T(1024)S(1)} %bitcast.96, f32[512]{0:T(512)S(1)} %add_rsqrt_fusion.1, f32[512]{0:T(512)S(1)} %broadcast_multiply_fusion.1, f32[3072]{0:T(1024)S(1)} %copy-done.11), kind=kLoop, calls=%fused_computation.13 | loop fusion | flops 9437184 | bytes 9478144 | tf_op jit(solution)/shard_map/convert_element_type | solution.py:98
  229.5 3.1 %copy.87 = bf16[3072,5,64]{2,0,1:T(8,128)(2,1)} copy(bf16[3072,5,64]{0,2,1:T(8,128)(2,1)S(1)} %copy-done.5) | data formatting | bytes 3932160 | tf_op jit(solution)/shard_map/reshape | solution.py:132
  232.6 4.7 %copy.88 = bf16[3072,5,64]{2,0,1:T(8,128)(2,1)} copy(bf16[3072,5,64]{0,2,1:T(8,128)(2,1)} %collective-permute-done) | data formatting | bytes 3932160 | tf_op jit(solution)/shard_map/ppermute | solution.py:18
  237.3 3.6 %broadcast_select_fusion.1 = (bf16[3072,5,64]{2,0,1:T(8,128)(2,1)S(1)}, bf16[3072,5,64]{2,0,1:T(8,128)(2,1)S(1)}) fusion(bf16[3072,5,64]{2,0,1:T(8,128)(2,1)} %copy.87, bf16[3072,5,64]{2,0,1:T(8,128)(2,1)} %copy.88, pred[]{:T(512)S(6)} %eq.14), kind=kLoop, calls=%fused_computation.17 | loop fusion | flops 1966080 | bytes 7864321 | tf_op jit(solution)/shard_map/jit(_where)/select_n | solution.py:21
  240.9 3.3 %pad_maximum_fusion.2 = (bf16[3072,2,128]{2,0,1:T(8,128)(2,1)S(1)}, bf16[3072,2,128]{2,0,1:T(8,128)(2,1)}) fusion(bf16[3072,5,64]{2,0,1:T(8,128)(2,1)S(1)} %get-tuple-element.12, bf16[3072,5,64]{2,0,1:T(8,128)(2,1)S(1)} %get-tuple-element.11), kind=kLoop, calls=%fused_computation.27 | loop fusion | flops 6291456 | bytes 7077888 | tf_op jit(solution)/shard_map/slice | solution.py:134
  244.4 2.6 copy.93
  247.0 1.6 copy.91
  248.6 3.5 %fusion.27 = bf16[16,2,16,128]{3,2,1,0:T(8,128)(2,1)S(1)} fusion(bf16[16,2,16,3072]{3,2,1,0:T(8,128)(2,1)} %bitcast.80, bf16[3072,5,64]{2,0,1:T(8,128)(2,1)} %copy-done.3, bf16[3072,5,64]{2,0,1:T(8,128)(2,1)} %copy-done.2), kind=kOutput, calls=%fused_computation.42 | convolution fusion | flops 404226048 | bytes 7208960 | tf_op jit(solution)/shard_map/dot_general | solution.py:170
  252.4 1.0 convolution_convert_fusion
  253.5 2.8 convert_reduce_fusion
  256.2 4.0 %fusion.43 = f32[512,256]{1,0:T(8,128)S(1)} fusion(bf16[3072,256]{0,1:T(8,128)(2,1)S(1)} %bitcast.83, bf16[3072,512]{1,0:T(8,128)(2,1)} %all-gather.3.cloned.1.call-done, f32[3072]{0:T(1024)S(1)} %bitcast.99, f32[3072]{0:T(1024)S(1)} %bitcast.97, f32[512]{0:T(512)S(1)} %get-tuple-element.27, f32[512]{0:T(512)S(1)} %get-tuple-element.26), kind=kOutput, calls=%fused_computation.58 | convolution fusion | flops 814743552 | bytes 5271552 | tf_op jit(solution)/shard_map/dot_general | solution.py:152
  260.3 2.1 fusion.19
  263.1 1.0 fusion.24
  264.1 3.6 %all-to-all-start.1 = ((bf16[16,16,128]{2,1,0:T(8,128)(2,1)}), bf16[16,16,128]{2,1,0:T(8,128)(2,1)S(1)}, u32[]{:S(2)}, u32[]{:S(2)}) async-start(bf16[16,16,128]{2,1,0:T(8,128)(2,1)} %bitcast.24), calls=%async_computation.1 | async-start | bytes 131072 | tf_op jit(solution)/shard_map/all_to_all | solution.py:200
  267.7 6.8 %all-to-all-done.1 = bf16[16,16,128]{2,1,0:T(8,128)(2,1)S(1)} async-done(((bf16[16,16,128]{2,1,0:T(8,128)(2,1)}), bf16[16,16,128]{2,1,0:T(8,128)(2,1)S(1)}, u32[]{:S(2)}, u32[]{:S(2)}) %all-to-all-start.1) | async-done | bytes 65568 | tf_op jit(solution)/shard_map/all_to_all | solution.py:200
  274.6 3.8 %fusion.51 = f32[16,3072]{1,0:T(8,128)S(1)} fusion(bf16[1024,3072]{1,0:T(8,128)(2,1)} %param.30, bf16[2,16,1024]{2,1,0:T(8,128)(2,1)S(1)} %bitcast.89, s32[]{:T(128)S(6)} %select_n.47), kind=kOutput, calls=%fused_computation.73 | convolution fusion | flops 100663296 | bytes 6520836 | tf_op jit(solution)/shard_map/dot_general | solution.py:205
  278.4 0.9 convolution_add_fusion
  279.2 5.5 %collective-permute-done.1 = f32[16,3072]{1,0:T(8,128)S(1)} collective-permute-done((f32[16,3072]{1,0:T(8,128)S(1)}, f32[16,3072]{1,0:T(8,128)S(1)}, u32[]{:S(2)}, u32[]{:S(2)}) %collective-permute-start.1) | collective-permute-done | bytes 196640 | tf_op jit(solution)/shard_map/ppermute | solution.py:215
  284.8 3.7 %fusion.12 = bf16[16,3072]{1,0:T(8,128)(2,1)S(1)} fusion(f32[16,3072]{1,0:T(8,128)S(1)} %convolution_add_fusion, f32[16,3072]{1,0:T(8,128)S(1)} %collective-permute-done.1, bf16[1024,3072]{1,0:T(8,128)(2,1)} %param.30, f32[3072]{0:T(1024)S(1)} %copy-done.14, f32[3072]{0:T(1024)S(1)} %bitcast.94, bf16[2,16,1024]{2,1,0:T(8,128)(2,1)S(1)} %bitcast.90, ...), kind=kOutput, calls=%fused_computation.23 | convolution fusion | flops 100909056 | bytes 6840324 | tf_op jit(solution)/shard_map/dot_general | solution.py:210
  (89 shorter events, 5.6 us)
Async XLA Ops:
  6.5 108.8 %copy-start = (bf16[3,3,3,16,512]{4,3,2,1,0:T(8,128)(2,1)S(1)}, bf16[3,3,3,16,512]{4,3,2,1,0:T(8,128)(2,1)}, u32[]{:S(2)}) copy-start(bf16[3,3,3,16,512]{4,3,2,1,0:T(8,128)(2,1)} %param.19) | copy-start | bytes 1327108
  11.3 10.1 %copy-start.19 = (s32[512]{0:T(512)S(1)}, s32[512]{0:T(512)}, u32[]{:S(2)}) copy-start(s32[512]{0:T(512)} %param.25) | copy-start | bytes 6148
  13.9 196.8 %all-to-all-start = ((bf16[16,192,320]{2,1,0:T(8,128)(2,1)}), bf16[16,192,320]{2,1,0:T(8,128)(2,1)}, u32[]{:S(2)}, u32[]{:S(2)}) async-start(bf16[16,192,320]{2,1,0:T(8,128)(2,1)} %copy.85), calls=%async_computation | async-start | bytes 4718592 | tf_op jit(solution)/shard_map/all_to_all | solution.py:131
  21.4 9.3 %copy-start.12 = (bf16[8,2,4,512]{3,2,1,0:T(4,128)(2,1)S(1)}, bf16[8,2,4,512]{3,2,1,0:T(4,128)(2,1)}, u32[]{:S(2)}) copy-start(bf16[8,2,4,512]{3,2,1,0:T(4,128)(2,1)} %param.16) | copy-start | bytes 196612
  21.4 93.8 %copy-start.15 = (f32[512]{0:T(512)S(1)}, f32[512]{0:T(512)}, u32[]{:S(2)}) copy-start(f32[512]{0:T(512)} %param.18) | copy-start | bytes 6148
  21.4 93.8 %copy-start.16 = (f32[512]{0:T(512)S(1)}, f32[512]{0:T(512)}, u32[]{:S(2)}) copy-start(f32[512]{0:T(512)} %param.17) | copy-start | bytes 6148
  21.4 167.0 %copy-start.18 = (f32[16]{0:T(128)S(1)}, f32[16]{0:T(128)}, u32[]{:S(2)}) copy-start(f32[16]{0:T(128)} %param.20) | copy-start | bytes 196
  21.4 232.0 %all-gather.3.cloned.1.call-start = ((), (), s32[]{:S(2)}) async-start(), calls=%async_computation.2 | async-start | bytes 3342336 | tf_op jit(solution)/shard_map/all_gather | solution.py:142
  30.6 158.9 %copy-start.7 = (bf16[64,3072]{1,0:T(8,128)(2,1)S(1)}, bf16[64,3072]{1,0:T(8,128)(2,1)}, u32[]{:S(2)}) copy-start(bf16[64,3072]{1,0:T(8,128)(2,1)} %param.21) | copy-start | bytes 1179652
  30.6 158.9 %copy-start.11 = (f32[3072]{0:T(1024)S(1)}, f32[3072]{0:T(1024)}, u32[]{:S(2)}) copy-start(f32[3072]{0:T(1024)} %param.22) | copy-start | bytes 36868
  189.5 3.7 %copy-start.10 = (bf16[512,64]{1,0:T(8,128)(2,1)}, bf16[512,64]{1,0:T(8,128)(2,1)S(1)}, u32[]{:S(2)}) copy-start(bf16[512,64]{1,0:T(8,128)(2,1)S(1)} %reshape.100) | copy-start | bytes 196612
  189.6 3.6 %copy-start.17 = (f32[2,192]{1,0:T(2,128)S(1)}, f32[2,192]{1,0:T(2,128)}, u32[]{:S(2)}) copy-start(f32[2,192]{1,0:T(2,128)} %param.28) | copy-start | bytes 4612
  218.4 4.7 %copy-start.13 = (f32[3,3072]{1,0:T(4,128)S(1)}, f32[3,3072]{1,0:T(4,128)}, u32[]{:S(2)}) copy-start(f32[3,3072]{1,0:T(4,128)} %param.23) | copy-start | bytes 110596
  218.4 14.2 %collective-permute-start = (bf16[3072,5,64]{0,2,1:T(8,128)(2,1)}, bf16[3072,5,64]{0,2,1:T(8,128)(2,1)}, u32[]{:S(2)}, u32[]{:S(2)}) collective-permute-start(bf16[3072,5,64]{0,2,1:T(8,128)(2,1)} %reshape.103), channel_id=1, source_target_pairs={{0,2},{2,0},{4,6},{6,4},{8,10},{10,8},{12,14},{14,12},{16,18},{18,... | collective-permute-start | bytes 5898248 | tf_op jit(solution)/shard_map/ppermute | solution.py:18
  223.2 6.3 %copy-start.5 = (bf16[3072,5,64]{0,2,1:T(8,128)(2,1)S(1)}, bf16[3072,5,64]{0,2,1:T(8,128)(2,1)}, u32[]{:S(2)}) copy-start(bf16[3072,5,64]{0,2,1:T(8,128)(2,1)} %reshape.103) | copy-start | bytes 5898244
  240.9 3.4 %copy-start.2 = (bf16[3072,5,64]{2,0,1:T(8,128)(2,1)}, bf16[3072,5,64]{2,0,1:T(8,128)(2,1)S(1)}, u32[]{:S(2)}) copy-start(bf16[3072,5,64]{2,0,1:T(8,128)(2,1)S(1)} %get-tuple-element.11) | copy-start | bytes 5898244
  240.9 3.5 %copy-start.3 = (bf16[3072,5,64]{2,0,1:T(8,128)(2,1)}, bf16[3072,5,64]{2,0,1:T(8,128)(2,1)S(1)}, u32[]{:S(2)}) copy-start(bf16[3072,5,64]{2,0,1:T(8,128)(2,1)S(1)} %get-tuple-element.12) | copy-start | bytes 5898244
  248.6 3.6 %copy-start.4 = (bf16[512,3072]{1,0:T(8,128)(2,1)S(1)}, bf16[512,3072]{1,0:T(8,128)(2,1)}, u32[]{:S(2)}) copy-start(bf16[512,3072]{1,0:T(8,128)(2,1)} %add_convert_fusion) | copy-start | bytes 9437188
  248.6 3.8 %copy-start.9 = (bf16[3072,2,128]{0,2,1:T(8,128)(2,1)S(1)}, bf16[3072,2,128]{0,2,1:T(8,128)(2,1)}, u32[]{:S(2)}) copy-start(bf16[3072,2,128]{0,2,1:T(8,128)(2,1)} %copy.91) | copy-start | bytes 4718596
  252.4 3.9 %copy-start.8 = (bf16[3072,2,128]{0,2,1:T(8,128)(2,1)S(1)}, bf16[3072,2,128]{0,2,1:T(8,128)(2,1)}, u32[]{:S(2)}) copy-start(bf16[3072,2,128]{0,2,1:T(8,128)(2,1)} %copy.93) | copy-start | bytes 4718596
  256.2 4.0 %copy-start.6 = (bf16[3072,512]{1,0:T(8,128)(2,1)S(1)}, bf16[3072,512]{1,0:T(8,128)(2,1)}, u32[]{:S(2)}) copy-start(bf16[3072,512]{1,0:T(8,128)(2,1)} %all-gather.3.cloned.1.call-done) | copy-start | bytes 9437188
  264.1 20.7 %copy-start.14 = (f32[3072]{0:T(1024)S(1)}, f32[3072]{0:T(1024)}, u32[]{:S(2)}) copy-start(f32[3072]{0:T(1024)} %param.31) | copy-start | bytes 36868
  264.1 10.5 %all-to-all-start.1 = ((bf16[16,16,128]{2,1,0:T(8,128)(2,1)}), bf16[16,16,128]{2,1,0:T(8,128)(2,1)S(1)}, u32[]{:S(2)}, u32[]{:S(2)}) async-start(bf16[16,16,128]{2,1,0:T(8,128)(2,1)} %bitcast.24), calls=%async_computation.1 | async-start | bytes 131072 | tf_op jit(solution)/shard_map/all_to_all | solution.py:200
  274.6 14.6 %copy-start.1 = (bf16[3,3,3,16,512]{4,3,2,1,0:T(8,128)(2,1)S(1)}, bf16[3,3,3,16,512]{4,3,2,1,0:T(8,128)(2,1)}, u32[]{:S(2)}) copy-start(bf16[3,3,3,16,512]{4,3,2,1,0:T(8,128)(2,1)} %param.19) | copy-start | bytes 1327108
  278.4 6.4 %collective-permute-start.1 = (f32[16,3072]{1,0:T(8,128)S(1)}, f32[16,3072]{1,0:T(8,128)S(1)}, u32[]{:S(2)}, u32[]{:S(2)}) collective-permute-start(f32[16,3072]{1,0:T(8,128)S(1)} %fusion.51), channel_id=1, source_target_pairs={{0,1},{1,0},{2,3},{3,2},{4,5},{5,4},{6,7},{7,6},{8,9},{9,8},{10,11... | collective-permute-start | bytes 589832 | tf_op jit(solution)/shard_map/ppermute | solution.py:215
Sparse Core Ops, SparseCore 0:
  30.8 66.3 all-gather.2

commit v2 on v1

--- a/solution.py
+++ b/solution.py
@@ -1,6 +1,10 @@
+import functools
+
 import jax
 import jax.numpy as jnp
 from jax import lax
+from jax.experimental import pallas as pl
+from jax.experimental.pallas import tpu as pltpu
 from jax.sharding import PartitionSpec as P
 
 HD = 128
@@ -10,18 +14,190 @@
 eps_norm = 1e-06
 
 
-def group_gather(piece, group, dim):
-    if group == 1:
-        return piece
-    count = lax.axis_size("seq")
-    if group == 2:
-        other = lax.ppermute(piece, "seq", [(i, i ^ 1) for i in range(count)])
-        first = lax.axis_index("seq") % 2 == 0
-        return jnp.concatenate(
-            [jnp.where(first, piece, other), jnp.where(first, other, piece)], axis=dim
-        )
-    members = [list(range(i, i + group)) for i in range(0, count, group)]
-    return lax.all_gather(piece, "seq", axis=dim, tiled=True, axis_index_groups=members)
+MESH = pl.DeviceIdType.MESH
+
+
+def share_kernel(seq_n, head_n, x_ref, out_ref, local_sem, send_sem, recv_sem):
+    count = seq_n * head_n
+    me = lax.axis_index("seq") * head_n + lax.axis_index("head")
+
+    def place(index):
+        return (lax.div(index, head_n), lax.rem(index, head_n))
+
+    barrier = pltpu.get_barrier_semaphore()
+
+    def greet(off, carry):
+        pl.semaphore_signal(
+            barrier, inc=1, device_id=place(lax.rem(me + off, count)), device_id_type=MESH
+        )
+        return carry
+
+    lax.fori_loop(1, count, greet, 0)
+    pl.semaphore_wait(barrier, count - 1)
+
+    def copy(off, slot):
+        return pltpu.make_async_remote_copy(
+            src_ref=x_ref,
+            dst_ref=out_ref.at[slot],
+            send_sem=send_sem.at[off],
+            recv_sem=recv_sem.at[off],
+            device_id=place(lax.rem(me + off, count)),
+            device_id_type=MESH,
+        )
+
+    def send(off, carry):
+        copy(off, me).start()
+        return carry
+
+    lax.fori_loop(1, count, send, 0)
+    own = pltpu.make_async_copy(x_ref, out_ref.at[me], local_sem)
+    own.start()
+    own.wait()
+
+    def finish(off, carry):
+        copy(off, me).wait_send()
+        copy(off, lax.rem(me + count - off, count)).wait_recv()
+        return carry
+
+    lax.fori_loop(1, count, finish, 0)
+
+
+def share(x, collective_id):
+    seq_n, head_n = lax.axis_size("seq"), lax.axis_size("head")
+    count = seq_n * head_n
+    return pl.pallas_call(
+        functools.partial(share_kernel, seq_n, head_n),
+        out_shape=jax.ShapeDtypeStruct((count, *x.shape), x.dtype),
+        in_specs=[pl.BlockSpec(memory_space=pltpu.VMEM)],
+        out_specs=pl.BlockSpec(memory_space=pltpu.VMEM),
+        scratch_shapes=[
+            pltpu.SemaphoreType.DMA,
+            pltpu.SemaphoreType.DMA((count,)),
+            pltpu.SemaphoreType.DMA((count,)),
+        ],
+        compiler_params=pltpu.CompilerParams(collective_id=collective_id, has_side_effects=True),
+    )(x)
+
+
+def weights_kernel(
+    heads_here,
+    group,
+    wq_ref,
+    wt_ref,
+    ctx_ref,
+    w_ref,
+    full_ref,
+    local_sem,
+    send_sem,
+    recv_sem,
+    pass_send,
+    pass_recv,
+):
+    s, h = lax.axis_index("seq"), lax.axis_index("head")
+    mine, place = lax.div(s, group), lax.rem(s, group)
+    width = heads_here * HD
+    barrier = pltpu.get_barrier_semaphore()
+    for off in range(1, heads_here):
+        peer = lax.rem(mine + off, heads_here) * group + place
+        pl.semaphore_signal(barrier, inc=1, device_id=(peer, h), device_id_type=MESH)
+    for off in range(1, group):
+        peer = mine * group + lax.rem(place + off, group)
+        pl.semaphore_signal(barrier, inc=1, device_id=(peer, h), device_id_type=MESH)
+    pl.semaphore_wait(barrier, heads_here - 1 + group - 1)
+
+    def pieces(head, slot):
+        out = []
+        for i in range(5):
+            ref, at = (wq_ref, i) if i < 3 else (wt_ref, i - 3)
+            start = pl.multiple_of(at * width + head * HD, HD)
+            out.append((ref.at[:, pl.ds(start, HD)], w_ref.at[slot, :, pl.ds(i * HD, HD)]))
+        out.append((ctx_ref, full_ref.at[slot]))
+        return out
+
+    def first(off, slot):
+        head = lax.rem(mine + off, heads_here)
+        return [
+            pltpu.make_async_remote_copy(
+                src_ref=src,
+                dst_ref=dst,
+                send_sem=send_sem.at[off, i],
+                recv_sem=recv_sem.at[off, i],
+                device_id=(head * group + place, h),
+                device_id_type=MESH,
+            )
+            for i, (src, dst) in enumerate(pieces(head, slot))
+        ]
+
+    def second(off, piece, slot):
+        peer = mine * group + lax.rem(place + off, group)
+        return [
+            pltpu.make_async_remote_copy(
+                src_ref=ref.at[slot],
+                dst_ref=ref.at[slot],
+                send_sem=pass_send.at[off, piece, i],
+                recv_sem=pass_recv.at[off, piece, i],
+                device_id=(peer, h),
+                device_id_type=MESH,
+            )
+            for i, ref in enumerate((w_ref, full_ref))
+        ]
+
+    for off in range(1, heads_here):
+        for copy in first(off, s):
+            copy.start()
+    own = [
+        pltpu.make_async_copy(src, dst, local_sem.at[i])
+        for i, (src, dst) in enumerate(pieces(mine, s))
+    ]
+    for copy in own:
+        copy.start()
+    for copy in own:
+        copy.wait()
+    for piece in range(heads_here):
+        slot = lax.rem(mine + heads_here - piece, heads_here) * group + place
+        if piece > 0:
+            for copy in first(piece, slot):
+                copy.wait_recv()
+        for off in range(1, group):
+            for copy in second(off, piece, slot):
+                copy.start()
+    for off in range(1, heads_here):
+        for copy in first(off, s):
+            copy.wait_send()
+    for piece in range(heads_here):
+        from_group = lax.rem(mine + heads_here - piece, heads_here) * group
+        for off in range(1, group):
+            for copy in second(off, piece, from_group + place):
+                copy.wait_send()
+            for copy in second(off, piece, from_group + lax.rem(place + group - off, group)):
+                copy.wait_recv()
+
+
+def gather_weights(w_qkv, w_text, own_context):
+    seq_n = lax.axis_size("seq")
+    depth, _, head_width = w_qkv.shape
+    heads_here = head_width // HD
+    group = seq_n // heads_here
+    text_count = own_context.shape[1]
+    anywhere = pl.BlockSpec(memory_space=pl.ANY)
+    sems = pltpu.SemaphoreType.DMA
+    return pl.pallas_call(
+        functools.partial(weights_kernel, heads_here, group),
+        out_shape=(
+            jax.ShapeDtypeStruct((seq_n, depth, 5 * HD), w_qkv.dtype),
+            jax.ShapeDtypeStruct((seq_n, depth, text_count), own_context.dtype),
+        ),
+        in_specs=[anywhere] * 3,
+        out_specs=(anywhere, anywhere),
+        scratch_shapes=[
+            sems((6,)),
+            sems((heads_here, 6)),
+            sems((heads_here, 6)),
+            sems((group, heads_here, 2)),
+            sems((group, heads_here, 2)),
+        ],
+        compiler_params=pltpu.CompilerParams(collective_id=2, has_side_effects=True),
+    )(w_qkv.reshape(depth, 3 * head_width), w_text.reshape(depth, 2 * head_width), own_context)
 
 
 def group_norm(features, gn_gain, gn_bias):
@@ -32,7 +208,8 @@
         [jnp.sum(values, axis=(0, 1, 2)), jnp.sum(values * values, axis=(0, 1, 2))]
     )
     sums = jnp.sum(chan_sums.reshape(2, GN_GROUPS, per_group), axis=2)
-    sums = lax.psum(sums, ("seq", "head"))
+    block = jnp.pad(sums, ((0, 6), (0, 128 - GN_GROUPS)))
+    sums = jnp.sum(share(block, 0), axis=0)[:2, :GN_GROUPS]
     cell_count = (
         frame_count * row_count * col_count * per_group * lax.axis_size("seq") * lax.axis_size("head")
     )
@@ -75,7 +252,7 @@
         preferred_element_type=jnp.float32,
     )[0]
     flat = shares.reshape(-1, 128)
-    parts = lax.all_gather(flat, ("seq", "head"), axis=0, tiled=False)
+    parts = share(flat, 1)
     parts = parts.reshape(
         seq_n, head_n, frame_count, row_count + 2, (col_count + 2) * chans
     )
@@ -123,15 +300,7 @@
     depth, _, head_width = w_qkv.shape
     heads_here = head_width // HD
     group = seq_n // heads_here
-    cols = head_width // seq_n
     text_count = text_ids.shape[0]
-
-    both = jnp.concatenate([w_qkv, w_text], axis=1).reshape(depth, 5, seq_n, cols)
-    both = both.transpose(2, 0, 1, 3).reshape(seq_n, depth, 5 * cols)
-    both = lax.all_to_all(both, "seq", split_axis=0, concat_axis=0, tiled=True)
-    both = both.reshape(seq_n * depth, 5, cols)
-    both = group_gather(both, group, 2)
-    w_query, w_image, w_text_full = both[:, 0], both[:, 1:3], both[:, 3:5]
 
     chosen = (
         lax.broadcasted_iota(jnp.int32, (text_table.shape[1], text_count), 0) == text_ids[None, :]
@@ -139,7 +308,9 @@
     own_context = jnp.dot(text_table, chosen, preferred_element_type=jnp.float32).astype(
         jnp.bfloat16
     )
-    context = lax.all_gather(own_context, "seq", axis=0, tiled=True).astype(jnp.float32)
+    weights, context = gather_weights(w_qkv, w_text, own_context)
+    weights = weights.reshape(width_full, 5 * HD)
+    context = context.reshape(width_full, text_count).astype(jnp.float32)
     mod = lax.all_gather(text_mod, "seq", axis=1, tiled=True)
     text_mean = jnp.sum(context, axis=0) / width_full
     text_square = jnp.sum(context * context, axis=0) / width_full
@@ -147,7 +318,7 @@
     text_normed = (context - text_mean) * text_scale * (1.0 + mod[1][:, None]) + mod[0][:, None]
     text_high = text_normed.astype(jnp.bfloat16)
     text_low = (text_normed - text_high.astype(jnp.float32)).astype(jnp.bfloat16)
-    w_text_flat = w_text_full.reshape(width_full, 2 * HD)
+    w_text_flat = weights[:, 3 * HD :]
     text_kv = sum(
         lax.dot_general(
             part, w_text_flat, (((0,), (0,)), ((), ())), preferred_element_type=jnp.float32
@@ -164,10 +335,8 @@
 
     def project(rows):
         modulated = modulate(rows, patch_weight, patch_bias, image_mod)
-        kv = jnp.dot(
-            modulated, w_image.reshape(width_full, 2 * HD), preferred_element_type=jnp.float32
-        )
-        query = jnp.dot(modulated, w_query, preferred_element_type=jnp.float32)
+        qkv = jnp.dot(modulated, weights[:, : 3 * HD], preferred_element_type=jnp.float32)
+        query, kv = qkv[:, :HD], qkv[:, HD:]
         query = lax.dynamic_index_in_dim(
             query.reshape(-1, group, part_rows, HD), my_part, axis=1, keepdims=False
         )

time: 297 us -> 204 us (0.69)
  blocking collectives: 169 us -> 23.6 us
  Pallas kernels: 0 us -> 86.2 us
  starting transfers between devices: 11.4 us -> 30.8 us
  local copies, waits for them, and re-layouts: 29.8 us -> 10.6 us
  between operations: 14.6 us -> 1.01 us
  matrix products: 37.4 us -> 27.4 us
  other arithmetic: 21.1 us -> 11.9 us
    pallas_call x0 -> x3, Pallas kernels: none -> 86.2 us  [the longest x1 59.7 us: gather_weights(): pl.pallas_call(functools.partial(weights_kernel, heads_here, group), out_...]
    psum x1 -> x0, blocking collectives: 83.9 us -> none  [group_norm(): sums = lax.psum(sums, ('seq', 'head'))]
    all_gather x1 -> x0, blocking collectives: 68.1 us -> none  [all_patches(): parts = lax.all_gather(flat, ('seq', 'head'), axis=0, tiled=False)]
    all_to_all x1, starting transfers between devices: 3.63 us -> 29.2 us  [body(): lax.all_to_all(attended, 'seq', split_axis=0, concat_axis=0, tiled=True)]
    reshape x3 -> x1, local copies, waits for them, and re-layouts: 9.46 us -> 1.09 us  [gather_weights(): w_qkv.reshape(depth, 3 * head_width)]
    all_to_all x1 -> x0, starting transfers between devices: 7.4 us -> none  [body(): both = lax.all_to_all(both, 'seq', split_axis=0, concat_axis=0, tiled=True)]
    all_gather x1, blocking collectives: 17.4 us -> 23.6 us  [body(): mod = lax.all_gather(text_mod, 'seq', axis=1, tiled=True)]
    ppermute x1 -> x0, local copies, waits for them, and re-layouts: 4.68 us -> none  [group_gather(): other = lax.ppermute(piece, 'seq', [(i, i ^ 1) for i in range(count)])]
  transfers between devices with their start and end apart: 5 -> 2, of which waited for: 2 -> 2; matrix products, arithmetic and copies ran while one was open for 21% -> 0% of each run, Pallas kernels for 0% -> 0%
where the time goes in v2:
time: 204 us; the launch traced here: 203 us
  Pallas kernels  86.2 us (42%)
  starting transfers between devices  30.8 us (15%)
  matrix products  27.4 us (13%)
  blocking collectives  23.6 us (12%)
  other arithmetic  11.9 us (6%)
  waiting for transfers between devices  11.5 us (6%)
  local copies, waits for them, and re-layouts  10.6 us (5%)
    pallas_call x1, Pallas kernels, gather_weights(): pl.pallas_call(functools.partial(weights_kernel, heads_here, group), out_...  59.7 us
    all_to_all x1, starting transfers between devices, body(): lax.all_to_all(attended, 'seq', split_axis=0, concat_axis=0, tiled=True)  29.2 us
    pallas_call x2, Pallas kernels, share(): pl.pallas_call(functools.partial(share_kernel, seq_n, head_n), out_shape=...  26.4 us
    all_gather x1, blocking collectives, body(): mod = lax.all_gather(text_mod, 'seq', axis=1, tiled=True)  23.6 us
    dot_general x1, matrix products, body(): jnp.dot(text_table, chosen, preferred_element_type=jnp.float32)  9.2 us
    all_to_all x1, waiting for transfers between devices, body(): lax.all_to_all(attended, 'seq', split_axis=0, concat_axis=0, tiled=True)  6.89 us
    ppermute x1, waiting for transfers between devices, body(): projected = here + lax.ppermute(away, 'head', [(0, 1), (1, 0)]) + out_bias  4.62 us
    conv_general_dilated x1, matrix products, all_patches(): lax.conv_general_dilated(padded[None], conv_weight, (1, 1, 1), ((0, 0), (...  4.24 us
  transfers between devices with their start and end apart: 2, of which 2 were waited for; matrix products, arithmetic and copies ran while one was open for 0% of the time, Pallas kernels for 0%

profile of v2, /device:TPU:0, one launch (start us, length us, event | category | flops | bytes accessed | tf_op | source)
XLA Modules:
  0.0 203.0 jit_solution(7266547748437557972)
XLA Ops:
  0.0 1.1 convert_reduce_fusion.1
  1.3 0.6 pad.20.x_ref
  2.0 12.0 %shard_map.154 = f32[32,8,128]{2,1,0:T(8,128)} custom-call(f32[8,128]{1,0:T(8,128)} %pad.20.x_ref), custom_call_target="tpu_custom_call" | custom-call | tf_op jit(solution)/shard_map/pallas_call | solution.py:68
  13.9 0.9 reduce_sum.84
  15.2 1.0 fusion.45
  16.2 4.2 %convolution_reduce_fusion = f32[8,4,6,16]{3,2,1,0:T(8,128)S(1)} fusion(bf16[3,3,3,16,512]{4,3,2,1,0:T(8,128)(2,1)S(1)} %copy-done, bf16[1,10,2,4,512]{4,3,2,1,0:T(4,128)(2,1)S(1)} %maximum_bitcast_fusion), kind=kOutput, calls=%fused_computation.33 | convolution fusion | flops 28311552 | bytes 536576 | tf_op jit(solution)/shard_map/conv_general_dilated | solution.py:246
  20.5 0.7 reshape_squeeze.3.x_ref
  21.2 14.5 %shard_map.155 = f32[32,24,128]{2,1,0:T(8,128)} custom-call(f32[24,128]{1,0:T(8,128)} %reshape_squeeze.3.x_ref), custom_call_target="tpu_custom_call" | custom-call | tf_op jit(solution)/shard_map/pallas_call | solution.py:68
  35.7 1.3 reshape.96
  38.0 0.7 tile.2
  38.7 23.6 %all-gather = f32[16,192,2]{1,2,0:T(2,128)S(1)} all-gather(f32[1,192,2]{1,2,0:T(2,128)} %bitcast.104), channel_id=1, replica_groups=mesh['seq'=16,'head'=2] {'seq'}, dimensions={0}, use_global_device_ids=true | all-gather | bytes 26112 | tf_op jit(solution)/shard_map/all_gather | solution.py:314
  62.5 1.0 fusion.63
  64.3 1.1 copy.46
  65.4 1.1 copy.44
  66.5 9.2 %fusion.24.ctx_ref = bf16[192,512]{1,0:T(8,128)(2,1)} fusion(bf16[192,16384]{1,0:T(8,128)(2,1)} %param.27, s32[512]{0:T(512)S(1)} %copy-done.8), kind=kOutput, calls=%fused_computation.31 | convolution fusion | flops 3229712384 | bytes 6490112 | tf_op jit(solution)/shard_map/dot_general | solution.py:308
  75.7 59.7 %shard_map.156 = (bf16[16,192,640]{2,1,0:T(8,128)(2,1)}, bf16[16,192,512]{2,1,0:T(8,128)(2,1)}) custom-call(bf16[192,3072]{1,0:T(8,128)(2,1)} %bitcast.83, bf16[192,2048]{1,0:T(8,128)(2,1)} %bitcast.84, bf16[192,512]{1,0:T(8,128)(2,1)} %fusion.24.ctx_ref), custom_call_target="tpu_custom_call" | custom-call | tf_op jit(solution)/shard_map/pallas_call | solution.py:184
  135.5 2.8 %convert_reduce_fusion = (f32[512]{0:T(512)S(1)}, f32[512]{0:T(512)S(1)}) fusion(bf16[16,192,512]{2,1,0:T(8,128)(2,1)} %get-tuple-element.8), kind=kLoop, calls=%fused_computation.13 | loop fusion | flops 6290432 | bytes 3149824 | tf_op jit(solution)/shard_map/reduce_sum | solution.py:315
  138.3 1.0 add_reduce_fusion
  139.3 2.6 %copy-done.1 = f32[512,3072]{1,0:T(8,128)} copy-done((f32[512,3072]{1,0:T(8,128)}, f32[512,3072]{1,0:T(8,128)S(1)}, u32[]{:S(2)}) %copy-start.1) | copy-done | bytes 6291480
  142.0 1.0 multiply_reduce_fusion.1
  143.0 3.5 %fusion.5 = (bf16[3072,512]{1,0:T(8,128)(2,1)S(1)}, bf16[3072,512]{1,0:T(8,128)(2,1)S(1)}) fusion(bf16[16,192,512]{2,1,0:T(8,128)(2,1)} %get-tuple-element.8, f32[3072]{0:T(1024)S(1)} %bitcast.100, f32[3072]{0:T(1024)S(1)} %bitcast.99, f32[512]{0:T(512)S(1)} %get-tuple-element.30, f32[512]{0:T(512)S(1)} %get-tuple-element.29), kind=kLoop, calls=%fused_computation.12 | loop fusion | flops 14155776 | bytes 9465856 | tf_op jit(solution)/shard_map/convert_element_type | solution.py:319
  146.5 1.0 fusion.12
  147.6 1.1 fusion.20
  148.7 1.9 fusion.10
  151.4 1.0 fusion.25
  152.4 29.2 %all-to-all-start = ((bf16[16,16,128]{2,1,0:T(8,128)(2,1)}), bf16[16,16,128]{2,1,0:T(8,128)(2,1)S(1)}, u32[]{:S(2)}, u32[]{:S(2)}) async-start(bf16[16,16,128]{2,1,0:T(8,128)(2,1)} %bitcast.18), calls=%async_computation | async-start | bytes 131072 | tf_op jit(solution)/shard_map/all_to_all | solution.py:369
  181.6 6.9 %all-to-all-done = bf16[16,16,128]{2,1,0:T(8,128)(2,1)S(1)} async-done(((bf16[16,16,128]{2,1,0:T(8,128)(2,1)}), bf16[16,16,128]{2,1,0:T(8,128)(2,1)S(1)}, u32[]{:S(2)}, u32[]{:S(2)}) %all-to-all-start) | async-done | bytes 65568 | tf_op jit(solution)/shard_map/all_to_all | solution.py:369
  188.5 3.7 %fusion.46 = f32[16,3072]{1,0:T(8,128)S(1)} fusion(bf16[1024,3072]{1,0:T(8,128)(2,1)} %param.30, bf16[2,16,1024]{2,1,0:T(8,128)(2,1)S(1)} %bitcast.94, s32[]{:T(128)S(6)} %select_n.30), kind=kOutput, calls=%fused_computation.65 | convolution fusion | flops 100663296 | bytes 6520836 | tf_op jit(solution)/shard_map/dot_general | solution.py:374
  192.2 1.6 collective-permute-start
  194.0 4.6 %collective-permute-done = f32[16,3072]{1,0:T(8,128)S(1)} collective-permute-done((f32[16,3072]{1,0:T(8,128)S(1)}, f32[16,3072]{1,0:T(8,128)S(1)}, u32[]{:S(2)}, u32[]{:S(2)}) %collective-permute-start) | collective-permute-done | bytes 196640 | tf_op jit(solution)/shard_map/ppermute | solution.py:384
  198.6 3.7 %fusion.9 = bf16[16,3072]{1,0:T(8,128)(2,1)S(1)} fusion(f32[16,3072]{1,0:T(8,128)S(1)} %convolution_add_fusion, f32[16,3072]{1,0:T(8,128)S(1)} %collective-permute-done, bf16[1024,3072]{1,0:T(8,128)(2,1)} %param.30, f32[3072]{0:T(1024)S(1)} %copy-done.7, f32[3072]{0:T(1024)S(1)} %bitcast.101, bf16[2,16,1024]{2,1,0:T(8,128)(2,1)S(1)} %bitcast.95, ...), kind=kOutput, calls=%fused_computation.19 | convolution fusion | flops 100909056 | bytes 6840324 | tf_op jit(solution)/shard_map/dot_general | solution.py:379
  202.3 0.7 reshape.105
  (55 shorter events, 3.1 us)
Async XLA Ops:
  0.0 16.2 %copy-start = (bf16[3,3,3,16,512]{4,3,2,1,0:T(8,128)(2,1)S(1)}, bf16[3,3,3,16,512]{4,3,2,1,0:T(8,128)(2,1)}, u32[]{:S(2)}) copy-start(bf16[3,3,3,16,512]{4,3,2,1,0:T(8,128)(2,1)} %param.19) | copy-start | bytes 1327108
  0.0 64.3 %copy-start.5 = (bf16[192,2,1024]{2,1,0:T(2,128)(2,1)S(1)}, bf16[192,2,1024]{2,1,0:T(2,128)(2,1)}, u32[]{:S(2)}) copy-start(bf16[192,2,1024]{2,1,0:T(2,128)(2,1)} %param.29) | copy-start | bytes 2359300
  0.0 65.4 %copy-start.4 = (bf16[192,3,1024]{2,0,1:T(8,128)(2,1)S(1)}, bf16[192,3,1024]{2,0,1:T(8,128)(2,1)}, u32[]{:S(2)}) copy-start(bf16[192,3,1024]{2,0,1:T(8,128)(2,1)} %param.24) | copy-start | bytes 3538948
  0.0 66.5 %copy-start.8 = (s32[512]{0:T(512)S(1)}, s32[512]{0:T(512)}, u32[]{:S(2)}) copy-start(s32[512]{0:T(512)} %param.25) | copy-start | bytes 6148
  66.5 71.7 %copy-start.3 = (bf16[64,3072]{1,0:T(8,128)(2,1)S(1)}, bf16[64,3072]{1,0:T(8,128)(2,1)}, u32[]{:S(2)}) copy-start(bf16[64,3072]{1,0:T(8,128)(2,1)} %param.21) | copy-start | bytes 1179652
  66.5 71.7 %copy-start.6 = (f32[3072]{0:T(1024)S(1)}, f32[3072]{0:T(1024)}, u32[]{:S(2)}) copy-start(f32[3072]{0:T(1024)} %param.22) | copy-start | bytes 36868
  139.3 2.7 %copy-start.1 = (f32[512,3072]{1,0:T(8,128)}, f32[512,3072]{1,0:T(8,128)S(1)}, u32[]{:S(2)}) copy-start(f32[512,3072]{1,0:T(8,128)S(1)} %get-tuple-element.32) | copy-start | bytes 18874372
  142.9 3.6 %copy-start.2 = (bf16[16,192,640]{2,1,0:T(8,128)(2,1)S(1)}, bf16[16,192,640]{2,1,0:T(8,128)(2,1)}, u32[]{:S(2)}) copy-start(bf16[16,192,640]{2,1,0:T(8,128)(2,1)} %get-tuple-element.7) | copy-start | bytes 11796484
  143.0 5.7 %slice-start = ((s8[6291456]{0:T(1024)(128)(4,1)}), s8[4194304]{0:T(1024)(128)(4,1)S(1)}, s32[]{:S(2)}) async-start(s8[6291456]{0:T(1024)(128)(4,1)} %bitcast.81), calls=%async_computation.1 | async-start | bytes 8388608
  146.5 2.1 %slice-start.1 = ((s8[6291456]{0:T(1024)(128)(4,1)}), s8[2097152]{0:T(1024)(128)(4,1)S(1)}, s32[]{:S(2)}) async-start(s8[6291456]{0:T(1024)(128)(4,1)} %bitcast.81), calls=%async_computation.2 | async-start | bytes 4194304
  150.5 48.1 %copy-start.7 = (f32[3072]{0:T(1024)S(1)}, f32[3072]{0:T(1024)}, u32[]{:S(2)}) copy-start(f32[3072]{0:T(1024)} %param.31) | copy-start | bytes 36868
  152.4 36.1 %all-to-all-start = ((bf16[16,16,128]{2,1,0:T(8,128)(2,1)}), bf16[16,16,128]{2,1,0:T(8,128)(2,1)S(1)}, u32[]{:S(2)}, u32[]{:S(2)}) async-start(bf16[16,16,128]{2,1,0:T(8,128)(2,1)} %bitcast.18), calls=%async_computation | async-start | bytes 131072 | tf_op jit(solution)/shard_map/all_to_all | solution.py:369
  192.2 6.4 %collective-permute-start = (f32[16,3072]{1,0:T(8,128)S(1)}, f32[16,3072]{1,0:T(8,128)S(1)}, u32[]{:S(2)}, u32[]{:S(2)}) collective-permute-start(f32[16,3072]{1,0:T(8,128)S(1)} %fusion.46), channel_id=1, source_target_pairs={{0,1},{1,0},{2,3},{3,2},{4,5},{5,4},{6,7},{7,6},{8,9},{9,8},{10,11... | collective-permute-start | bytes 589832 | tf_op jit(solution)/shard_map/ppermute | solution.py:384

commit v3 on v2

--- a/solution.py
+++ b/solution.py
@@ -17,23 +17,31 @@
 MESH = pl.DeviceIdType.MESH
 
 
-def share_kernel(seq_n, head_n, x_ref, out_ref, local_sem, send_sem, recv_sem):
+def place_of(index, head_n):
+    return (lax.div(index, head_n), lax.rem(index, head_n))
+
+
+def greet_all(seq_n, head_n):
     count = seq_n * head_n
     me = lax.axis_index("seq") * head_n + lax.axis_index("head")
-
-    def place(index):
-        return (lax.div(index, head_n), lax.rem(index, head_n))
-
     barrier = pltpu.get_barrier_semaphore()
 
     def greet(off, carry):
         pl.semaphore_signal(
-            barrier, inc=1, device_id=place(lax.rem(me + off, count)), device_id_type=MESH
+            barrier,
+            inc=1,
+            device_id=place_of(lax.rem(me + off, count), head_n),
+            device_id_type=MESH,
         )
         return carry
 
     lax.fori_loop(1, count, greet, 0)
     pl.semaphore_wait(barrier, count - 1)
+
+
+def start_share(seq_n, head_n, x_ref, out_ref, local_sem, send_sem, recv_sem):
+    count = seq_n * head_n
+    me = lax.axis_index("seq") * head_n + lax.axis_index("head")
 
     def copy(off, slot):
         return pltpu.make_async_remote_copy(
@@ -41,7 +49,7 @@
             dst_ref=out_ref.at[slot],
             send_sem=send_sem.at[off],
             recv_sem=recv_sem.at[off],
-            device_id=place(lax.rem(me + off, count)),
+            device_id=place_of(lax.rem(me + off, count), head_n),
             device_id_type=MESH,
         )
 
@@ -52,14 +60,80 @@
     lax.fori_loop(1, count, send, 0)
     own = pltpu.make_async_copy(x_ref, out_ref.at[me], local_sem)
     own.start()
+
+    def finish():
+        own.wait()
+
+        def wait(off, carry):
+            copy(off, me).wait_send()
+            copy(off, lax.rem(me + count - off, count)).wait_recv()
+            return carry
+
+        lax.fori_loop(1, count, wait, 0)
+
+    return finish
+
+
+def share_kernel(seq_n, head_n, x_ref, out_ref, local_sem, send_sem, recv_sem):
+    greet_all(seq_n, head_n)
+    start_share(seq_n, head_n, x_ref, out_ref, local_sem, send_sem, recv_sem)()
+
+
+def swap_kernel(seq_n, x_ref, out_ref, local_sem, send_sem, recv_sem):
+    me, h = lax.axis_index("seq"), lax.axis_index("head")
+    barrier = pltpu.get_barrier_semaphore()
+
+    def greet(off, carry):
+        pl.semaphore_signal(
+            barrier, inc=1, device_id=(lax.rem(me + off, seq_n), h), device_id_type=MESH
+        )
+        return carry
+
+    lax.fori_loop(1, seq_n, greet, 0)
+    pl.semaphore_wait(barrier, seq_n - 1)
+
+    def copy(off, slot):
+        peer = lax.rem(me + off, seq_n)
+        return pltpu.make_async_remote_copy(
+            src_ref=x_ref.at[peer],
+            dst_ref=out_ref.at[slot],
+            send_sem=send_sem.at[off],
+            recv_sem=recv_sem.at[off],
+            device_id=(peer, h),
+            device_id_type=MESH,
+        )
+
+    def send(off, carry):
+        copy(off, me).start()
+        return carry
+
+    lax.fori_loop(1, seq_n, send, 0)
+    own = pltpu.make_async_copy(x_ref.at[me], out_ref.at[me], local_sem)
+    own.start()
     own.wait()
 
-    def finish(off, carry):
+    def wait(off, carry):
         copy(off, me).wait_send()
-        copy(off, lax.rem(me + count - off, count)).wait_recv()
+        copy(off, lax.rem(me + seq_n - off, seq_n)).wait_recv()
         return carry
 
-    lax.fori_loop(1, count, finish, 0)
+    lax.fori_loop(1, seq_n, wait, 0)
+
+
+def swap(x):
+    seq_n = lax.axis_size("seq")
+    return pl.pallas_call(
+        functools.partial(swap_kernel, seq_n),
+        out_shape=jax.ShapeDtypeStruct(x.shape, x.dtype),
+        in_specs=[pl.BlockSpec(memory_space=pltpu.VMEM)],
+        out_specs=pl.BlockSpec(memory_space=pltpu.VMEM),
+        scratch_shapes=[
+            pltpu.SemaphoreType.DMA,
+            pltpu.SemaphoreType.DMA((seq_n,)),
+            pltpu.SemaphoreType.DMA((seq_n,)),
+        ],
+        compiler_params=pltpu.CompilerParams(collective_id=1, has_side_effects=True),
+    )(x)
 
 
 def share(x, collective_id):
@@ -85,25 +159,26 @@
     wq_ref,
     wt_ref,
     ctx_ref,
+    x_ref,
     w_ref,
     full_ref,
+    parts_ref,
     local_sem,
     send_sem,
     recv_sem,
     pass_send,
     pass_recv,
+    share_local,
+    share_send,
+    share_recv,
 ):
     s, h = lax.axis_index("seq"), lax.axis_index("head")
     mine, place = lax.div(s, group), lax.rem(s, group)
     width = heads_here * HD
-    barrier = pltpu.get_barrier_semaphore()
-    for off in range(1, heads_here):
-        peer = lax.rem(mine + off, heads_here) * group + place
-        pl.semaphore_signal(barrier, inc=1, device_id=(peer, h), device_id_type=MESH)
-    for off in range(1, group):
-        peer = mine * group + lax.rem(place + off, group)
-        pl.semaphore_signal(barrier, inc=1, device_id=(peer, h), device_id_type=MESH)
-    pl.semaphore_wait(barrier, heads_here - 1 + group - 1)
+    greet_all(lax.axis_size("seq"), lax.axis_size("head"))
+    finish_share = start_share(
+        lax.axis_size("seq"), lax.axis_size("head"), x_ref, parts_ref, share_local, share_send, share_recv
+    )
 
     def pieces(head, slot):
         out = []
@@ -171,13 +246,15 @@
                 copy.wait_send()
             for copy in second(off, piece, from_group + lax.rem(place + group - off, group)):
                 copy.wait_recv()
-
-
-def gather_weights(w_qkv, w_text, own_context):
+    finish_share()
+
+
+def gather_weights(w_qkv, w_text, own_context, shares):
     seq_n = lax.axis_size("seq")
     depth, _, head_width = w_qkv.shape
     heads_here = head_width // HD
     group = seq_n // heads_here
+    count = seq_n * lax.axis_size("head")
     text_count = own_context.shape[1]
     anywhere = pl.BlockSpec(memory_space=pl.ANY)
     sems = pltpu.SemaphoreType.DMA
@@ -186,21 +263,25 @@
         out_shape=(
             jax.ShapeDtypeStruct((seq_n, depth, 5 * HD), w_qkv.dtype),
             jax.ShapeDtypeStruct((seq_n, depth, text_count), own_context.dtype),
+            jax.ShapeDtypeStruct((count, *shares.shape), shares.dtype),
         ),
-        in_specs=[anywhere] * 3,
-        out_specs=(anywhere, anywhere),
+        in_specs=[anywhere] * 3 + [pl.BlockSpec(memory_space=pltpu.VMEM)],
+        out_specs=(anywhere, anywhere, pl.BlockSpec(memory_space=pltpu.VMEM)),
         scratch_shapes=[
             sems((6,)),
             sems((heads_here, 6)),
             sems((heads_here, 6)),
             sems((group, heads_here, 2)),
             sems((group, heads_here, 2)),
+            sems,
+            sems((count,)),
+            sems((count,)),
         ],
         compiler_params=pltpu.CompilerParams(collective_id=2, has_side_effects=True),
-    )(w_qkv.reshape(depth, 3 * head_width), w_text.reshape(depth, 2 * head_width), own_context)
-
-
-def group_norm(features, gn_gain, gn_bias):
+    )(w_qkv.reshape(depth, 3 * head_width), w_text.reshape(depth, 2 * head_width), own_context, shares)
+
+
+def group_norm(features, gn_gain, gn_bias, text_mod):
     frame_count, row_count, col_count, chan_count = features.shape
     per_group = chan_count // GN_GROUPS
     values = features.astype(jnp.float32)
@@ -208,8 +289,17 @@
         [jnp.sum(values, axis=(0, 1, 2)), jnp.sum(values * values, axis=(0, 1, 2))]
     )
     sums = jnp.sum(chan_sums.reshape(2, GN_GROUPS, per_group), axis=2)
-    block = jnp.pad(sums, ((0, 6), (0, 128 - GN_GROUPS)))
-    sums = jnp.sum(share(block, 0), axis=0)[:2, :GN_GROUPS]
+    seq_n, head_n = lax.axis_size("seq"), lax.axis_size("head")
+    depth = text_mod.shape[1]
+    lines = -(-depth // 128)
+    mod = jnp.pad(text_mod, ((0, 0), (0, lines * 128 - depth))).reshape(2 * lines, 128)
+    block = jnp.concatenate([jnp.pad(sums, ((0, 0), (0, 128 - GN_GROUPS))), mod], axis=0)
+    block = jnp.pad(block, ((0, -block.shape[0] % 8), (0, 0)))
+    shared = share(block, 0)
+    sums = jnp.sum(shared[:, :2, :GN_GROUPS], axis=0)
+    mod = shared.reshape(seq_n, head_n, -1, 128)[:, 0, 2 : 2 + 2 * lines]
+    mod = mod.reshape(seq_n, 2, lines * 128)[:, :, :depth]
+    mod = mod.transpose(1, 0, 2).reshape(2, seq_n * depth)
     cell_count = (
         frame_count * row_count * col_count * per_group * lax.axis_size("seq") * lax.axis_size("head")
     )
@@ -218,7 +308,7 @@
     mean = jnp.repeat(mean, per_group)
     scale = jnp.repeat(scale, per_group)
     normed = (values - mean) * scale
-    return jax.nn.silu(normed * gn_gain + gn_bias).astype(jnp.bfloat16)
+    return jax.nn.silu(normed * gn_gain + gn_bias).astype(jnp.bfloat16), mod
 
 
 def join_rims(parts, block_dim, dim, unit):
@@ -238,10 +328,7 @@
     return core + jnp.pad(low, pad_low) + jnp.pad(high, pad_high)
 
 
-def all_patches(activated, conv_weight, conv_bias):
-    seq_n, head_n = lax.axis_size("seq"), lax.axis_size("head")
-    frame_count, row_count, col_count, _ = activated.shape
-    chans = conv_weight.shape[3]
+def conv_shares(activated, conv_weight):
     padded = jnp.concatenate([activated[:1], activated[:1], activated], axis=0)
     shares = lax.conv_general_dilated(
         padded[None],
@@ -251,8 +338,12 @@
         dimension_numbers=("NDHWC", "DHWOI", "NDHWC"),
         preferred_element_type=jnp.float32,
     )[0]
-    flat = shares.reshape(-1, 128)
-    parts = share(flat, 1)
+    return shares.reshape(-1, 128)
+
+
+def all_patches(parts, frame_count, row_count, col_count, conv_bias):
+    seq_n, head_n = lax.axis_size("seq"), lax.axis_size("head")
+    chans = conv_bias.shape[0]
     parts = parts.reshape(
         seq_n, head_n, frame_count, row_count + 2, (col_count + 2) * chans
     )
@@ -308,10 +399,11 @@
     own_context = jnp.dot(text_table, chosen, preferred_element_type=jnp.float32).astype(
         jnp.bfloat16
     )
-    weights, context = gather_weights(w_qkv, w_text, own_context)
+    activated, mod = group_norm(features, gn_gain, gn_bias, text_mod)
+    shares = conv_shares(activated, conv_weight)
+    weights, context, parts = gather_weights(w_qkv, w_text, own_context, shares)
     weights = weights.reshape(width_full, 5 * HD)
     context = context.reshape(width_full, text_count).astype(jnp.float32)
-    mod = lax.all_gather(text_mod, "seq", axis=1, tiled=True)
     text_mean = jnp.sum(context, axis=0) / width_full
     text_square = jnp.sum(context * context, axis=0) / width_full
     text_scale = lax.rsqrt(text_square - text_mean * text_mean + eps_norm)
@@ -326,8 +418,7 @@
         for part in (text_high, text_low)
     ).astype(jnp.bfloat16)
 
-    activated = group_norm(features, gn_gain, gn_bias)
-    patches = all_patches(activated, conv_weight, conv_bias)
+    patches = all_patches(parts, frame_count, row_count, col_count, conv_bias)
     own = patches.shape[0] // (seq_n * head_n)
     part_rows = head_n * own // group
     my_part = seq_i % group
@@ -366,21 +457,14 @@
     ).astype(jnp.bfloat16)
 
     attended = attended.reshape(seq_n, part_rows, HD)
-    attended = lax.all_to_all(attended, "seq", split_axis=0, concat_axis=0, tiled=True)
+    attended = swap(attended)
     attended = attended.reshape(heads_here, group, part_rows, HD).transpose(1, 2, 0, 3)
     attended = attended.reshape(head_n * own, head_width)
     if head_n == 2:
-        halves = attended.reshape(2, own, head_width)
-        away = jnp.dot(
-            lax.dynamic_index_in_dim(halves, 1 - head_i, 0, keepdims=False),
-            w_out,
-            preferred_element_type=jnp.float32,
-        )
-        here = jnp.dot(
-            lax.dynamic_index_in_dim(halves, head_i, 0, keepdims=False),
-            w_out,
-            preferred_element_type=jnp.float32,
-        )
+        halves = jnp.dot(attended, w_out, preferred_element_type=jnp.float32)
+        halves = halves.reshape(2, own, width_full)
+        away = lax.dynamic_index_in_dim(halves, 1 - head_i, 0, keepdims=False)
+        here = lax.dynamic_index_in_dim(halves, head_i, 0, keepdims=False)
         projected = here + lax.ppermute(away, "head", [(0, 1), (1, 0)]) + out_bias
     else:
         projected = (

time: 204 us -> 175 us (0.86)
  Pallas kernels: 86.2 us -> 118 us
  starting transfers between devices: 30.8 us -> 0.62 us
  blocking collectives: 23.6 us -> 0 us
  waiting for transfers between devices: 11.5 us -> 6.36 us
  local copies, waits for them, and re-layouts: 10.6 us -> 14.1 us
  matrix products: 27.4 us -> 24.1 us
    pallas_call x0 -> x1, Pallas kernels: none -> 32.6 us  [swap(): pl.pallas_call(functools.partial(swap_kernel, seq_n), out_shape=jax.Shape...]
    all_to_all x1 -> x0, starting transfers between devices: 29.2 us -> none  [body(): lax.all_to_all(attended, 'seq', split_axis=0, concat_axis=0, tiled=True)]
    all_gather x1 -> x0, blocking collectives: 23.6 us -> none  [body(): mod = lax.all_gather(text_mod, 'seq', axis=1, tiled=True)]
    pallas_call x2 -> x1, Pallas kernels: 26.4 us -> 11.9 us  [share(): pl.pallas_call(functools.partial(share_kernel, seq_n, head_n), out_shape=...]
    pallas_call x1, Pallas kernels: 59.7 us -> 73.5 us  [gather_weights(): pl.pallas_call(functools.partial(weights_kernel, heads_here, group), out_...]
    all_to_all x1 -> x0, waiting for transfers between devices: 6.89 us -> none  [body(): lax.all_to_all(attended, 'seq', split_axis=0, concat_axis=0, tiled=True)]
    dot_general x2 -> x1, matrix products: 7.44 us -> 4 us  [body(): halves = jnp.dot(attended, w_out, preferred_element_type=jnp.float32)]
    unnamed x24 -> x21, local copies, waits for them, and re-layouts: 3.91 us -> 4.95 us
  transfers between devices with their start and end apart: 2 -> 1, of which waited for: 2 -> 1; matrix products, arithmetic and copies ran while one was open for 0% -> 0% of each run, Pallas kernels for 0% -> 0%
where the time goes in v3:
time: 175 us
  Pallas kernels  118 us (67%)
  matrix products  24.1 us (14%)
  local copies, waits for them, and re-layouts  14.1 us (8%)
  other arithmetic  10.7 us (6%)
  waiting for transfers between devices  6.36 us (4%)
    pallas_call x1, Pallas kernels, gather_weights(): pl.pallas_call(functools.partial(weights_kernel, heads_here, group), out_...  73.5 us
    pallas_call x1, Pallas kernels, swap(): pl.pallas_call(functools.partial(swap_kernel, seq_n), out_shape=jax.Shape...  32.6 us
    pallas_call x1, Pallas kernels, share(): pl.pallas_call(functools.partial(share_kernel, seq_n, head_n), out_shape=...  11.9 us
    dot_general x1, matrix products, body(): jnp.dot(text_table, chosen, preferred_element_type=jnp.float32)  9.18 us
    ppermute x1, waiting for transfers between devices, body(): projected = here + lax.ppermute(away, 'head', [(0, 1), (1, 0)]) + out_bias  6.36 us
    unnamed x21, local copies, waits for them, and re-layouts  4.95 us
    conv_general_dilated x1, matrix products, conv_shares(): lax.conv_general_dilated(padded[None], conv_weight, (1, 1, 1), ((0, 0), (...  4.24 us
    dot_general x1, matrix products, body(): halves = jnp.dot(attended, w_out, preferred_element_type=jnp.float32)  4 us
  transfers between devices with their start and end apart: 1, of which 1 were waited for; matrix products, arithmetic and copies ran while one was open for 0% of the time, Pallas kernels for 0%

profile of v3, /device:TPU:0, one launch (start us, length us, event | category | flops | bytes accessed | tf_op | source)
XLA Modules:
  0.0 174.9 jit_solution(13961882786533268738)
XLA Ops:
  0.0 0.7 pad.29
  0.8 0.9 convert_reduce_fusion.1
  1.9 0.6 pad.30.x_ref
  2.5 11.9 %shard_map.154 = f32[32,8,128]{2,1,0:T(8,128)} custom-call(f32[8,128]{1,0:T(8,128)} %pad.30.x_ref), custom_call_target="tpu_custom_call" | custom-call | tf_op jit(solution)/shard_map/pallas_call | solution.py:142
  14.5 0.9 slice_reduce_fusion
  15.8 1.0 fusion.47
  16.8 4.2 %convolution_reduce_fusion = f32[8,4,6,16]{3,2,1,0:T(8,128)S(1)} fusion(bf16[3,3,3,16,512]{4,3,2,1,0:T(8,128)(2,1)S(1)} %copy-done, bf16[1,10,2,4,512]{4,3,2,1,0:T(4,128)(2,1)S(1)} %maximum_bitcast_fusion), kind=kOutput, calls=%fused_computation.30 | convolution fusion | flops 28311552 | bytes 536576 | tf_op jit(solution)/shard_map/conv_general_dilated | solution.py:333
  21.1 0.7 reshape_squeeze.6.x_ref
  21.8 2.3 %copy.37 = bf16[24,8,2,1024]{3,1,2,0:T(8,128)(2,1)} copy(bf16[24,8,2,1024]{3,2,1,0:T(2,128)(2,1)} %bitcast.92) | data formatting | bytes 1572864
  24.0 2.4 %copy.35 = bf16[3,24,8,1024]{3,2,0,1:T(8,128)(2,1)} copy(bf16[3,24,8,1024]{3,2,1,0:T(8,128)(2,1)} %bitcast.90) | data formatting | bytes 2359296 | tf_op jit(solution)/shard_map/reshape | solution.py:281
  26.4 9.2 %fusion.22.ctx_ref = bf16[192,512]{1,0:T(8,128)(2,1)} fusion(bf16[192,16384]{1,0:T(8,128)(2,1)} %param.27, s32[512]{0:T(512)} %param.25), kind=kOutput, calls=%fused_computation.28 | convolution fusion | flops 3229712384 | bytes 6490112 | tf_op jit(solution)/shard_map/dot_general | solution.py:399
  35.6 73.5 %shard_map.155 = (bf16[16,192,640]{2,1,0:T(8,128)(2,1)}, bf16[16,192,512]{2,1,0:T(8,128)(2,1)}, f32[32,24,128]{2,1,0:T(8,128)}) custom-call(bf16[192,3072]{1,0:T(8,128)(2,1)} %bitcast.85, bf16[192,2048]{1,0:T(8,128)(2,1)} %bitcast.86, bf16[192,512]{1,0:T(8,128)(2,1)} %fusion.22.ctx_ref, f32[24,128]{1,0:T(8,128)} %reshape_squeeze.6.x_ref), custom_call_target="tpu_custom_call" | custom-call | tf_op jit(solution)/shard_map/pallas_call | solution.py:261
  109.1 1.3 reshape.114
  110.5 0.2 fusion.57
  111.6 0.8 slice.121
  112.7 2.8 %convert_reduce_fusion = (f32[512]{0:T(512)S(1)}, f32[512]{0:T(512)S(1)}) fusion(bf16[16,192,512]{2,1,0:T(8,128)(2,1)} %get-tuple-element.10), kind=kLoop, calls=%fused_computation.15 | loop fusion | flops 6290432 | bytes 3149824 | tf_op jit(solution)/shard_map/reduce_sum | solution.py:407
  116.0 0.3 copy.29
  116.4 1.0 add_reduce_fusion
  117.5 2.6 %copy-done.1 = f32[512,3072]{1,0:T(8,128)} copy-done((f32[512,3072]{1,0:T(8,128)}, f32[512,3072]{1,0:T(8,128)S(1)}, u32[]{:S(2)}) %copy-start.1) | copy-done | bytes 6291480
  120.1 1.0 multiply_reduce_fusion.1
  121.2 3.3 %fusion.7 = (bf16[3072,512]{1,0:T(8,128)(2,1)S(1)}, bf16[3072,512]{1,0:T(8,128)(2,1)S(1)}) fusion(bf16[16,192,512]{2,1,0:T(8,128)(2,1)} %get-tuple-element.10, f32[3072]{0:T(1024)S(1)} %add.208, f32[3072]{0:T(1024)S(1)} %add.207, f32[512]{0:T(512)S(1)} %get-tuple-element.32, f32[512]{0:T(512)S(1)} %get-tuple-element.31), kind=kLoop, calls=%fused_computation.14 | loop fusion | flops 14155776 | bytes 9465856 | tf_op jit(solution)/shard_map/convert_element_type | solution.py:411
  124.5 1.0 fusion.10
  125.5 1.1 fusion.18
  126.6 2.0 %fusion.8 = bf16[512,384]{1,0:T(8,128)(2,1)S(1)} fusion(f32[512,3072]{1,0:T(8,128)S(1)} %bitcast.84, f32[3072]{0:T(1024)S(1)} %bitcast.101, f32[3072]{0:T(1024)S(1)} %bitcast.102, f32[512]{0:T(512)S(1)} %add_rsqrt_fusion.1, f32[512]{0:T(512)S(1)} %broadcast_multiply_fusion.1, f32[3072]{0:T(1024)S(1)} %copy-done.4, bf16[3072,640]{1,0:T(8,128)(2,1)S(1)} %bitcast.89), kind=kOutput, calls=%fused_computation.17 | convolution fusion | flops 1217396736 | bytes 9084928 | tf_op jit(solution)/shard_map/dot_general | solution.py:429
  128.7 0.4 fusion.62
  129.1 0.3 fusion.24
  129.4 1.0 fusion.23
  130.4 32.6 %shard_map.156 = bf16[16,16,128]{2,1,0:T(8,128)(2,1)} custom-call(bf16[16,16,128]{2,1,0:T(8,128)(2,1)} %bitcast.99), custom_call_target="tpu_custom_call" | custom-call | tf_op jit(solution)/shard_map/pallas_call | solution.py:125
  163.1 4.0 %fusion.2 = f32[2,16,3072]{2,1,0:T(8,128)S(1)} fusion(bf16[1024,3072]{1,0:T(8,128)(2,1)} %param.30, bf16[8,2,2,8,128]{4,3,2,1,0:T(8,128)(2,1)} %bitcast.97), kind=kOutput, calls=%fused_computation.3 | convolution fusion | flops 201326592 | bytes 6750208 | tf_op jit(solution)/shard_map/dot_general | solution.py:464
  167.1 0.6 collective-permute-start
  167.7 6.4 %collective-permute-done = f32[16,3072]{1,0:T(8,128)S(1)} collective-permute-done((f32[16,3072]{1,0:T(8,128)S(1)}, f32[16,3072]{1,0:T(8,128)S(1)}, u32[]{:S(2)}, u32[]{:S(2)}) %collective-permute-start) | collective-permute-done | bytes 196640 | tf_op jit(solution)/shard_map/ppermute | solution.py:468
  174.3 0.7 reshape.122
  (55 shorter events, 2.2 us)
Async XLA Ops:
  0.0 16.8 %copy-start = (bf16[3,3,3,16,512]{4,3,2,1,0:T(8,128)(2,1)S(1)}, bf16[3,3,3,16,512]{4,3,2,1,0:T(8,128)(2,1)}, u32[]{:S(2)}) copy-start(bf16[3,3,3,16,512]{4,3,2,1,0:T(8,128)(2,1)} %param.19) | copy-start | bytes 1327108
  26.4 85.1 %copy-start.7 = (f32[16]{0:T(128)S(1)}, f32[16]{0:T(128)}, u32[]{:S(2)}) copy-start(f32[16]{0:T(128)} %param.20) | copy-start | bytes 196
  26.4 85.2 %copy-start.5 = (f32[3,3072]{1,0:T(4,128)S(1)}, f32[3,3072]{1,0:T(4,128)}, u32[]{:S(2)}) copy-start(f32[3,3072]{1,0:T(4,128)} %param.23) | copy-start | bytes 110596
  35.6 80.8 %copy-start.3 = (bf16[64,3072]{1,0:T(8,128)(2,1)S(1)}, bf16[64,3072]{1,0:T(8,128)(2,1)}, u32[]{:S(2)}) copy-start(bf16[64,3072]{1,0:T(8,128)(2,1)} %param.21) | copy-start | bytes 1179652
  35.6 80.8 %copy-start.4 = (f32[3072]{0:T(1024)S(1)}, f32[3072]{0:T(1024)}, u32[]{:S(2)}) copy-start(f32[3072]{0:T(1024)} %param.22) | copy-start | bytes 36868
  117.5 2.7 %copy-start.1 = (f32[512,3072]{1,0:T(8,128)}, f32[512,3072]{1,0:T(8,128)S(1)}, u32[]{:S(2)}) copy-start(f32[512,3072]{1,0:T(8,128)S(1)} %get-tuple-element.34) | copy-start | bytes 18874372
  121.1 3.4 %copy-start.2 = (bf16[16,192,640]{2,1,0:T(8,128)(2,1)S(1)}, bf16[16,192,640]{2,1,0:T(8,128)(2,1)}, u32[]{:S(2)}) copy-start(bf16[16,192,640]{2,1,0:T(8,128)(2,1)} %get-tuple-element.9) | copy-start | bytes 11796484
  121.1 5.5 %slice-start = ((s8[6291456]{0:T(1024)(128)(4,1)}), s8[4194304]{0:T(1024)(128)(4,1)S(1)}, s32[]{:S(2)}) async-start(s8[6291456]{0:T(1024)(128)(4,1)} %bitcast.83), calls=%async_computation | async-start | bytes 8388608
  124.5 2.1 %slice-start.1 = ((s8[6291456]{0:T(1024)(128)(4,1)}), s8[2097152]{0:T(1024)(128)(4,1)S(1)}, s32[]{:S(2)}) async-start(s8[6291456]{0:T(1024)(128)(4,1)} %bitcast.83), calls=%async_computation.1 | async-start | bytes 4194304
  128.6 45.5 %copy-start.6 = (f32[3072]{0:T(1024)S(1)}, f32[3072]{0:T(1024)}, u32[]{:S(2)}) copy-start(f32[3072]{0:T(1024)} %param.31) | copy-start | bytes 36868
  167.1 7.0 %collective-permute-start = (f32[16,3072]{1,0:T(8,128)S(1)}, f32[16,3072]{1,0:T(8,128)S(1)}, u32[]{:S(2)}, u32[]{:S(2)}) collective-permute-start(f32[16,3072]{1,0:T(8,128)S(1)} %dynamic-slice_bitcast_fusion), channel_id=1, source_target_pairs={{0,1},{1,0},{2,3},{3,2},{4,5},{5,4},{6,7},{7,6},{8,9},{9,8},{10,11... | collective-permute-start | bytes 589832 | tf_op jit(solution)/shard_map/ppermute | solution.py:468

commit v4 on v3

--- a/solution.py
+++ b/solution.py
@@ -156,6 +156,7 @@
 def weights_kernel(
     heads_here,
     group,
+    halves,
     wq_ref,
     wt_ref,
     ctx_ref,
@@ -168,6 +169,8 @@
     recv_sem,
     pass_send,
     pass_recv,
+    over_send,
+    over_recv,
     share_local,
     share_send,
     share_recv,
@@ -175,18 +178,18 @@
     s, h = lax.axis_index("seq"), lax.axis_index("head")
     mine, place = lax.div(s, group), lax.rem(s, group)
     width = heads_here * HD
+    half = h if halves == 2 else 0
     greet_all(lax.axis_size("seq"), lax.axis_size("head"))
     finish_share = start_share(
         lax.axis_size("seq"), lax.axis_size("head"), x_ref, parts_ref, share_local, share_send, share_recv
     )
 
     def pieces(head, slot):
-        out = []
+        out = [(ctx_ref, full_ref.at[half, slot])]
         for i in range(5):
             ref, at = (wq_ref, i) if i < 3 else (wt_ref, i - 3)
             start = pl.multiple_of(at * width + head * HD, HD)
             out.append((ref.at[:, pl.ds(start, HD)], w_ref.at[slot, :, pl.ds(i * HD, HD)]))
-        out.append((ctx_ref, full_ref.at[slot]))
         return out
 
     def first(off, slot):
@@ -207,15 +210,26 @@
         peer = mine * group + lax.rem(place + off, group)
         return [
             pltpu.make_async_remote_copy(
-                src_ref=ref.at[slot],
-                dst_ref=ref.at[slot],
+                src_ref=ref,
+                dst_ref=ref,
                 send_sem=pass_send.at[off, piece, i],
                 recv_sem=pass_recv.at[off, piece, i],
                 device_id=(peer, h),
                 device_id_type=MESH,
             )
-            for i, ref in enumerate((w_ref, full_ref))
+            for i, ref in enumerate((w_ref.at[slot], full_ref.at[half, slot]))
         ]
+
+    def over(off, piece, side, slot):
+        peer = mine * group + lax.rem(place + off, group)
+        return pltpu.make_async_remote_copy(
+            src_ref=full_ref.at[side, slot],
+            dst_ref=full_ref.at[side, slot],
+            send_sem=over_send.at[off, piece],
+            recv_sem=over_recv.at[off, piece],
+            device_id=(peer, 1 - h),
+            device_id_type=MESH,
+        )
 
     for off in range(1, heads_here):
         for copy in first(off, s):
@@ -231,7 +245,13 @@
     for piece in range(heads_here):
         slot = lax.rem(mine + heads_here - piece, heads_here) * group + place
         if piece > 0:
-            for copy in first(piece, slot):
+            arriving = first(piece, slot)
+            arriving[0].wait_recv()
+        if halves == 2:
+            for off in range(group):
+                over(off, piece, h, slot).start()
+        if piece > 0:
+            for copy in arriving[1:]:
                 copy.wait_recv()
         for off in range(1, group):
             for copy in second(off, piece, slot):
@@ -246,10 +266,15 @@
                 copy.wait_send()
             for copy in second(off, piece, from_group + lax.rem(place + group - off, group)):
                 copy.wait_recv()
+        if halves == 2:
+            for off in range(group):
+                over(off, piece, h, from_group + place).wait_send()
+                there = from_group + lax.rem(place + group - off, group)
+                over(off, piece, 1 - h, there).wait_recv()
     finish_share()
 
 
-def gather_weights(w_qkv, w_text, own_context, shares):
+def gather_weights(w_qkv, w_text, own_context, shares, halves):
     seq_n = lax.axis_size("seq")
     depth, _, head_width = w_qkv.shape
     heads_here = head_width // HD
@@ -259,10 +284,10 @@
     anywhere = pl.BlockSpec(memory_space=pl.ANY)
     sems = pltpu.SemaphoreType.DMA
     return pl.pallas_call(
-        functools.partial(weights_kernel, heads_here, group),
+        functools.partial(weights_kernel, heads_here, group, halves),
         out_shape=(
             jax.ShapeDtypeStruct((seq_n, depth, 5 * HD), w_qkv.dtype),
-            jax.ShapeDtypeStruct((seq_n, depth, text_count), own_context.dtype),
+            jax.ShapeDtypeStruct((halves, seq_n, depth, text_count), own_context.dtype),
             jax.ShapeDtypeStruct((count, *shares.shape), shares.dtype),
         ),
         in_specs=[anywhere] * 3 + [pl.BlockSpec(memory_space=pltpu.VMEM)],
@@ -273,6 +298,8 @@
             sems((heads_here, 6)),
             sems((group, heads_here, 2)),
             sems((group, heads_here, 2)),
+            sems((group, heads_here)),
+            sems((group, heads_here)),
             sems,
             sems((count,)),
             sems((count,)),
@@ -393,19 +420,24 @@
     group = seq_n // heads_here
     text_count = text_ids.shape[0]
 
+    halves = 2 if head_n == 2 else 1
+    count_here = text_count // halves
+    ids_here = text_ids
+    if halves == 2:
+        ids_here = lax.dynamic_slice_in_dim(text_ids, head_i * count_here, count_here)
     chosen = (
-        lax.broadcasted_iota(jnp.int32, (text_table.shape[1], text_count), 0) == text_ids[None, :]
+        lax.broadcasted_iota(jnp.int32, (text_table.shape[1], count_here), 0) == ids_here[None, :]
     ).astype(jnp.bfloat16)
     own_context = jnp.dot(text_table, chosen, preferred_element_type=jnp.float32).astype(
         jnp.bfloat16
     )
     activated, mod = group_norm(features, gn_gain, gn_bias, text_mod)
     shares = conv_shares(activated, conv_weight)
-    weights, context, parts = gather_weights(w_qkv, w_text, own_context, shares)
+    weights, context, parts = gather_weights(w_qkv, w_text, own_context, shares, halves)
     weights = weights.reshape(width_full, 5 * HD)
-    context = context.reshape(width_full, text_count).astype(jnp.float32)
-    text_mean = jnp.sum(context, axis=0) / width_full
-    text_square = jnp.sum(context * context, axis=0) / width_full
+    context = context.reshape(halves, width_full, count_here).astype(jnp.float32)
+    text_mean = jnp.sum(context, axis=1, keepdims=True) / width_full
+    text_square = jnp.sum(context * context, axis=1, keepdims=True) / width_full
     text_scale = lax.rsqrt(text_square - text_mean * text_mean + eps_norm)
     text_normed = (context - text_mean) * text_scale * (1.0 + mod[1][:, None]) + mod[0][:, None]
     text_high = text_normed.astype(jnp.bfloat16)
@@ -413,10 +445,10 @@
     w_text_flat = weights[:, 3 * HD :]
     text_kv = sum(
         lax.dot_general(
-            part, w_text_flat, (((0,), (0,)), ((), ())), preferred_element_type=jnp.float32
+            part, w_text_flat, (((1,), (0,)), ((), ())), preferred_element_type=jnp.float32
         )
         for part in (text_high, text_low)
-    ).astype(jnp.bfloat16)
+    ).astype(jnp.bfloat16).reshape(text_count, 2 * HD)
 
     patches = all_patches(parts, frame_count, row_count, col_count, conv_bias)
     own = patches.shape[0] // (seq_n * head_n)

time: 175 us -> 178 us (1.017)
  Pallas kernels: 118 us -> 111 us
  local copies, waits for them, and re-layouts: 14.1 us -> 20.8 us
  matrix products: 24.1 us -> 30.3 us
  other arithmetic: 10.7 us -> 7.36 us
    pallas_call x1, Pallas kernels: 32.6 us -> 24.8 us  [swap(): pl.pallas_call(functools.partial(swap_kernel, seq_n), out_shape=jax.Shape...]
    convert_element_type x0 -> x1, local copies, waits for them, and re-layouts: none -> 5.4 us  [body(): context.reshape(halves, width_full, count_here).astype(jnp.float32)]
    dot_general x2, matrix products: 2.08 us -> 7.41 us  [body(): lax.dot_general(part, w_text_flat, (((1,), (0,)), ((), ())), preferred_el...]
    dot_general x1, matrix products: 1.96 us -> 5.35 us  [project(): jnp.dot(modulated, weights[:, :3 * HD], preferred_element_type=jnp.float32)]
    convert_element_type x1 -> x0, other arithmetic: 3.32 us -> none  [body(): text_high = text_normed.astype(jnp.bfloat16)]
    dot_general x1, matrix products: 9.18 us -> 6.71 us  [body(): jnp.dot(text_table, chosen, preferred_element_type=jnp.float32)]
    unnamed x21 -> x19, local copies, waits for them, and re-layouts: 4.95 us -> 5.53 us
where the time goes in v4:
time: 178 us; the launch traced here: 177 us
  Pallas kernels  111 us (62%)
  matrix products  30.3 us (17%)
  local copies, waits for them, and re-layouts  20.8 us (12%)
  other arithmetic  7.36 us (4%)
  waiting for transfers between devices  5.45 us (3%)
    pallas_call x1, Pallas kernels, gather_weights(): pl.pallas_call(functools.partial(weights_kernel, heads_here, group, halve...  74.3 us
    pallas_call x1, Pallas kernels, swap(): pl.pallas_call(functools.partial(swap_kernel, seq_n), out_shape=jax.Shape...  24.8 us
    pallas_call x1, Pallas kernels, share(): pl.pallas_call(functools.partial(share_kernel, seq_n, head_n), out_shape=...  12 us
    dot_general x2, matrix products, body(): lax.dot_general(part, w_text_flat, (((1,), (0,)), ((), ())), preferred_el...  7.41 us
    dot_general x1, matrix products, body(): jnp.dot(text_table, chosen, preferred_element_type=jnp.float32)  6.71 us
    unnamed x19, local copies, waits for them, and re-layouts  5.53 us
    ppermute x1, waiting for transfers between devices, body(): projected = here + lax.ppermute(away, 'head', [(0, 1), (1, 0)]) + out_bias  5.45 us
    convert_element_type x1, local copies, waits for them, and re-layouts, body(): context.reshape(halves, width_full, count_here).astype(jnp.float32)  5.4 us
  transfers between devices with their start and end apart: 1, of which 1 were waited for; matrix products, arithmetic and copies ran while one was open for 0% of the time, Pallas kernels for 0%

profile of v4, /device:TPU:0, one launch (start us, length us, event | category | flops | bytes accessed | tf_op | source)
XLA Modules:
  0.0 177.4 jit_solution(17869332625443314775)
XLA Ops:
  0.0 0.7 pad.29
  0.8 0.9 convert_reduce_fusion.1
  1.9 0.6 pad.30.x_ref
  2.5 12.0 %shard_map.154 = f32[32,8,128]{2,1,0:T(8,128)} custom-call(f32[8,128]{1,0:T(8,128)} %pad.30.x_ref), custom_call_target="tpu_custom_call" | custom-call | tf_op jit(solution)/shard_map/pallas_call | solution.py:142
  14.5 0.9 slice_reduce_fusion
  15.8 1.0 fusion.43
  16.8 4.2 %convolution_reduce_fusion = f32[8,4,6,16]{3,2,1,0:T(8,128)S(1)} fusion(bf16[3,3,3,16,512]{4,3,2,1,0:T(8,128)(2,1)S(1)} %copy-done, bf16[1,10,2,4,512]{4,3,2,1,0:T(4,128)(2,1)S(1)} %maximum_bitcast_fusion), kind=kOutput, calls=%fused_computation.29 | convolution fusion | flops 28311552 | bytes 536576 | tf_op jit(solution)/shard_map/conv_general_dilated | solution.py:360
  21.1 0.7 reshape_squeeze.6.x_ref
  21.8 2.3 %copy.40 = bf16[24,8,2,1024]{3,1,2,0:T(8,128)(2,1)} copy(bf16[24,8,2,1024]{3,2,1,0:T(2,128)(2,1)} %bitcast.81) | data formatting | bytes 1572864
  24.0 2.4 %copy.38 = bf16[3,24,8,1024]{3,2,0,1:T(8,128)(2,1)} copy(bf16[3,24,8,1024]{3,2,1,0:T(8,128)(2,1)} %bitcast.79) | data formatting | bytes 2359296 | tf_op jit(solution)/shard_map/reshape | solution.py:308
  26.4 0.8 dynamic_slice.17
  27.2 6.7 %fusion.19.ctx_ref = bf16[192,256]{1,0:T(8,128)(2,1)} fusion(bf16[192,16384]{1,0:T(8,128)(2,1)} %param.27, s32[256]{0:T(256)S(1)} %dynamic_slice.17), kind=kOutput, calls=%fused_computation.31 | convolution fusion | flops 1614856192 | bytes 6390784 | tf_op jit(solution)/shard_map/dot_general | solution.py:431
  33.9 74.3 %shard_map.155 = (bf16[16,192,640]{2,1,0:T(8,128)(2,1)}, bf16[2,16,192,256]{3,2,1,0:T(8,128)(2,1)}, f32[32,24,128]{2,1,0:T(8,128)}) custom-call(bf16[192,3072]{1,0:T(8,128)(2,1)} %bitcast.77, bf16[192,2048]{1,0:T(8,128)(2,1)} %bitcast.78, bf16[192,256]{1,0:T(8,128)(2,1)} %fusion.19.ctx_ref, f32[24,128]{1,0:T(8,128)} %reshape_squeeze.6.x_ref), custom_call_target="tpu_custom_call" | custom-call | tf_op jit(solution)/shard_map/pallas_call | solution.py:286
  108.2 1.3 reshape.124
  110.6 0.8 slice.121
  111.8 2.7 %convert_reduce_fusion = (f32[2,256]{1,0:T(2,128)S(1)}, f32[2,256]{1,0:T(2,128)S(1)}) fusion(bf16[2,16,192,256]{3,2,1,0:T(8,128)(2,1)} %get-tuple-element.10), kind=kLoop, calls=%fused_computation.14 | loop fusion | flops 6290432 | bytes 3149824 | tf_op jit(solution)/shard_map/reduce_sum | solution.py:439
  115.4 5.4 %copy.32 = f32[2,3072,256]{1,2,0:T(8,128)} copy(bf16[2,3072,256]{2,1,0:T(8,128)(2,1)} %bitcast.74) | data formatting | bytes 9437184 | tf_op jit(solution)/shard_map/convert_element_type | solution.py:438
  120.8 4.5 %fusion.5 = f32[2,256,256]{2,1,0:T(8,128)S(1)} fusion(f32[2,3072,256]{1,2,0:T(8,128)} %copy.32, f32[3072]{0:T(1024)S(1)} %add.217, f32[3072]{0:T(1024)S(1)} %add.216, f32[2,256]{1,0:T(2,128)S(1)} %get-tuple-element.30, f32[2,256]{1,0:T(2,128)S(1)} %get-tuple-element.29, bf16[3072,640]{1,0:T(8,128)(2,1)} %bitcast.93), kind=kOutput, calls=%fused_computation.13 | convolution fusion | flops 813170688 | bytes 8417280 | tf_op jit(solution)/shard_map/dot_general | solution.py:447
  125.4 0.6 slice-done.1
  126.0 2.9 %fusion.16 = bf16[2,256,256]{2,1,0:T(8,128)(2,1)S(1)} fusion(f32[2,256,256]{2,1,0:T(8,128)S(1)} %fusion.5, f32[2,3072,256]{1,2,0:T(8,128)S(1)} %bitcast.76, f32[3072]{0:T(1024)S(1)} %add.217, f32[3072]{0:T(1024)S(1)} %add.216, f32[2,256]{1,0:T(2,128)S(1)} %get-tuple-element.30, f32[2,256]{1,0:T(2,128)S(1)} %get-tuple-element.29, bf16[3072,640]{1,0:T(8,128)(2,1)} %bitcast.94), kind=kOutput, calls=%fused_computation.26 | convolution fusion | flops 818151424 | bytes 8679424 | tf_op jit(solution)/shard_map/dot_general | solution.py:447
  128.9 1.0 add_reduce_fusion
  129.9 2.6 %copy-done.1 = f32[512,3072]{1,0:T(8,128)} copy-done((f32[512,3072]{1,0:T(8,128)}, f32[512,3072]{1,0:T(8,128)S(1)}, u32[]{:S(2)}) %copy-start.1) | copy-done | bytes 6291480
  132.6 1.0 multiply_reduce_fusion.1
  133.6 5.3 %fusion.12 = bf16[512,384]{1,0:T(8,128)(2,1)S(1)} fusion(f32[512,3072]{1,0:T(8,128)} %copy-done.1, f32[3072]{0:T(1024)S(1)} %bitcast.91, f32[3072]{0:T(1024)S(1)} %bitcast.92, f32[512]{0:T(512)S(1)} %add_rsqrt_fusion.1, f32[512]{0:T(512)S(1)} %broadcast_multiply_fusion.1, f32[3072]{0:T(1024)S(1)} %copy-done.3, bf16[3072,640]{1,0:T(8,128)(2,1)} %bitcast.95), kind=kOutput, calls=%fused_computation.20 | convolution fusion | flops 1217396736 | bytes 9084928 | tf_op jit(solution)/shard_map/dot_general | solution.py:461
  139.1 0.4 fusion.58
  139.5 0.3 fusion.20
  139.8 1.0 fusion.18
  140.7 24.8 %shard_map.156 = bf16[16,16,128]{2,1,0:T(8,128)(2,1)} custom-call(bf16[16,16,128]{2,1,0:T(8,128)(2,1)} %bitcast.89), custom_call_target="tpu_custom_call" | custom-call | tf_op jit(solution)/shard_map/pallas_call | solution.py:125
  165.5 4.0 %fusion.2 = f32[2,16,3072]{2,1,0:T(8,128)S(1)} fusion(bf16[1024,3072]{1,0:T(8,128)(2,1)} %param.30, bf16[8,2,2,8,128]{4,3,2,1,0:T(8,128)(2,1)} %bitcast.86), kind=kOutput, calls=%fused_computation.3 | convolution fusion | flops 201326592 | bytes 6750208 | tf_op jit(solution)/shard_map/dot_general | solution.py:496
  169.6 1.5 collective-permute-start
  171.1 5.5 %collective-permute-done = f32[16,3072]{1,0:T(8,128)S(1)} collective-permute-done((f32[16,3072]{1,0:T(8,128)S(1)}, f32[16,3072]{1,0:T(8,128)S(1)}, u32[]{:S(2)}, u32[]{:S(2)}) %collective-permute-start) | collective-permute-done | bytes 196640 | tf_op jit(solution)/shard_map/ppermute | solution.py:500
  176.7 0.7 reshape.133
  (54 shorter events, 2.6 us)
Async XLA Ops:
  0.0 16.8 %copy-start = (bf16[3,3,3,16,512]{4,3,2,1,0:T(8,128)(2,1)S(1)}, bf16[3,3,3,16,512]{4,3,2,1,0:T(8,128)(2,1)}, u32[]{:S(2)}) copy-start(bf16[3,3,3,16,512]{4,3,2,1,0:T(8,128)(2,1)} %param.19) | copy-start | bytes 1327108
  27.2 83.3 %copy-start.6 = (f32[16]{0:T(128)S(1)}, f32[16]{0:T(128)}, u32[]{:S(2)}) copy-start(f32[16]{0:T(128)} %param.20) | copy-start | bytes 196
  27.2 83.4 %copy-start.4 = (f32[3,3072]{1,0:T(4,128)S(1)}, f32[3,3072]{1,0:T(4,128)}, u32[]{:S(2)}) copy-start(f32[3,3072]{1,0:T(4,128)} %param.23) | copy-start | bytes 110596
  120.8 4.5 %slice-start = ((s8[6291456]{0:T(1024)(128)(4,1)}), s8[4194304]{0:T(1024)(128)(4,1)S(1)}, s32[]{:S(2)}) async-start(s8[6291456]{0:T(1024)(128)(4,1)} %bitcast.75), calls=%async_computation | async-start | bytes 8388608
  120.8 5.1 %slice-start.1 = ((s8[6291456]{0:T(1024)(128)(4,1)}), s8[2097152]{0:T(1024)(128)(4,1)S(1)}, s32[]{:S(2)}) async-start(s8[6291456]{0:T(1024)(128)(4,1)} %bitcast.75), calls=%async_computation.1 | async-start | bytes 4194304
  125.9 2.9 %copy-start.2 = (bf16[64,3072]{1,0:T(8,128)(2,1)S(1)}, bf16[64,3072]{1,0:T(8,128)(2,1)}, u32[]{:S(2)}) copy-start(bf16[64,3072]{1,0:T(8,128)(2,1)} %param.21) | copy-start | bytes 1179652
  125.9 2.9 %copy-start.3 = (f32[3072]{0:T(1024)S(1)}, f32[3072]{0:T(1024)}, u32[]{:S(2)}) copy-start(f32[3072]{0:T(1024)} %param.22) | copy-start | bytes 36868
  129.9 2.7 %copy-start.1 = (f32[512,3072]{1,0:T(8,128)}, f32[512,3072]{1,0:T(8,128)S(1)}, u32[]{:S(2)}) copy-start(f32[512,3072]{1,0:T(8,128)S(1)} %get-tuple-element.32) | copy-start | bytes 18874372
  138.9 37.6 %copy-start.5 = (f32[3072]{0:T(1024)S(1)}, f32[3072]{0:T(1024)}, u32[]{:S(2)}) copy-start(f32[3072]{0:T(1024)} %param.31) | copy-start | bytes 36868
  169.6 7.0 %collective-permute-start = (f32[16,3072]{1,0:T(8,128)S(1)}, f32[16,3072]{1,0:T(8,128)S(1)}, u32[]{:S(2)}, u32[]{:S(2)}) collective-permute-start(f32[16,3072]{1,0:T(8,128)S(1)} %dynamic-slice_bitcast_fusion), channel_id=1, source_target_pairs={{0,1},{1,0},{2,3},{3,2},{4,5},{5,4},{6,7},{7,6},{8,9},{9,8},{10,11... | collective-permute-start | bytes 589832 | tf_op jit(solution)/shard_map/ppermute | solution.py:500
